TPU v7x, 32 devices: a whole 2x2x4 slice. The times are simulated.
32 devices in a mesh: sky: 16 (over z, y, x), band: 2 (over core).
Axes of the slice: x: 2, y: 2, z: 4, core: 2. Of those that a mesh axis runs over, the one named last changes fastest.
Arguments:
- stamps: bfloat16 [4096, 6, 2304], P('sky', 'band'), may hold values from 0 to 2
- stamp_gain: bfloat16 [4096], P('sky'), may hold values from 0.5 to 2
- stamp_invvar: bfloat16 [4096], P('sky'), may hold values from 1 to 10
- stamp_dest: int32 [4096, 1], P('sky'), may hold values from 0 to 15; in each aligned block of 256 rows (0 to 255, 256 to 511, ...) at most 32 rows name the same one
- stamp_obj: int32 [4096], P('sky'), may hold values from 0 to 63
- phi_tpl: bfloat16 [6, 16, 2304], P('band'), may hold values from 0 to 0.041503906
- psi_tpl: bfloat16 [6, 16, 2304], P('band'), may hold values from 0 to 0.041503906
- theta_init: float32 [16, 1024], P(None, 'sky'), may hold values from -3 to 3
- nb_id: int32 [1024, 4], P('sky'), may hold values from 0 to 1023, as said below
- nb_weight: float32 [1024, 4], P('sky'), may hold values from 0.2 to 0.8
Outputs:
- theta_fit: float32 [16, 1024], P(None, 'sky')
Inputs may be any that keep to these rules, and one draw needn't show every extreme that they name: `stamp_dest`: among the stamps of one index of sky no destination is named more than 32 times, a bound that some block reaches. `nb_id`: each neighbour is owned by the object's own index of sky or by the index just before or after it, cyclically.
All inputs are finite; a program needn't handle non-finite values.
Results may differ from a plain program's by a relative error of at most 0.0007.
Values may be sent and summed in bfloat16 or wider, within the bound.
No kernel may reach another device: no remote copies, remote signals or barrier semaphores. Data moves between devices by JAX's collectives and lax.ppermute only.
A program may use at most 128 MiB of HBM per device.

v0:
```python
import functools

import jax
import jax.numpy as jnp
import numpy as np
from jax import lax
from jax.experimental import pallas as pl
from jax.experimental.pallas import tpu as pltpu
from jax.sharding import PartitionSpec as P

ITERS = 3

ROBUST = 9.0
DAMPING = 0.1
PRIOR = 1.0
STEP_LIMIT = 0.5

LANES = 128
GROUP = 32
VMEM_LIMIT = 32 * 1024 * 1024

f32 = jnp.float32
bf16 = jnp.bfloat16
NT = (((1,), (1,)), ((), ()))
TN = (((0,), (0,)), ((), ()))
NN = (((1,), (0,)), ((), ()))


def dot(a, b, dims=NN, precision=None):
    return lax.dot_general(a, b, dims, precision=precision, preferred_element_type=f32)


def split3(x):
    first = x.astype(bf16)
    rest = x - first.astype(f32)
    second = rest.astype(bf16)
    third = (rest - second.astype(f32)).astype(bf16)
    return first, second, third


def iota(shape, dim):
    return lax.broadcasted_iota(jnp.int32, shape, dim)


@functools.lru_cache
def tables(size_k):
    pairs = [(k, l) for k in range(size_k) for l in range(k, size_k)]
    extra = len(pairs) - LANES
    assert 0 <= extra and extra + size_k <= GROUP
    left = np.zeros((size_k, 2 * LANES), np.float32)
    right = np.zeros((size_k, 2 * LANES), np.float32)
    grad = np.zeros((size_k, 2 * LANES), np.float32)
    full = np.zeros((size_k * size_k + size_k, 2 * LANES), np.float32)
    for m, (k, l) in enumerate(pairs):
        left[k, m] = 1.0
        right[l, m] = 1.0
        spots = [m] if m < LANES else [m + GROUP * g for g in range(LANES // GROUP)]
        full[k * size_k + l, spots] = 1.0
        full[l * size_k + k, spots] = 1.0
    for k in range(size_k):
        spot = LANES + extra + k
        grad[k, spot] = 1.0
        full[size_k * size_k + k, [spot + GROUP * g for g in range(LANES // GROUP)]] = 1.0
    return left, right, grad, full


def first_kernel(sizes, small_ref, theta_ref, nbi_ref, nbw_ref, pay_ref, sel_ref, inv_ref):
    n_sky, cap, obj_dev = sizes
    stamps = small_ref.shape[1]
    total = n_sky * cap
    dest = small_ref[0:1, :]
    obj = small_ref[1:2, :]
    along = jnp.broadcast_to(dest, (stamps, stamps))
    down = along.T
    before = iota((stamps, stamps), 0) < iota((stamps, stamps), 1)
    rank = jnp.sum(jnp.where(before & (along == down), 1.0, 0.0), axis=0, keepdims=True)
    place = dest.astype(jnp.int32) * cap + rank.astype(jnp.int32)
    sel = jnp.where(iota((total, stamps), 0) == place, 1.0, 0.0)
    sel_ref[...] = sel.astype(bf16)
    inv_ref[...] = jnp.broadcast_to(small_ref[3:4, :], (LANES, stamps)).T
    named = dot(jnp.broadcast_to(obj + 1.0, (8, stamps)), sel, NT, lax.Precision.HIGHEST)
    slot = iota((n_sky, total), 1)
    own = iota((n_sky, total), 0)
    spread = jnp.where((slot >= own * cap) & (slot < own * cap + cap), named[0:1, :], 0.0)
    turn = jnp.where(
        lax.rem(iota((total, LANES), 0), cap) == iota((total, LANES), 1), 1.0, 0.0
    )
    ids = dot(spread, turn, precision=lax.Precision.HIGHEST)
    size_k = theta_ref.shape[0]
    half = size_k // 2
    lane = iota((8, LANES), 1)
    row = iota((8, LANES), 0)
    theta = theta_ref[...]
    folded = jnp.concatenate([theta[:half], theta[half:]], axis=1)
    side = jnp.concatenate([nbi_ref[...].astype(f32), nbw_ref[...]], axis=1)
    side = jnp.concatenate([side, jnp.zeros((8 - side.shape[0], LANES), f32)], axis=0)
    del lane
    for d in range(n_sky):
        pay_ref[d, 0:8, :] = folded
        pay_ref[d, 8:16, :] = jnp.where(row == nbi_ref.shape[0], ids[d : d + 1, :], side)


def pair_kernel(phi_ref, psi_ref, left_ref, right_ref, grad_ref, tpl_ref, pair_ref, prow_ref):
    bands, size_k, pix = phi_ref.shape
    chunk = 256

    def step(c, carry):
        px = pl.ds(pl.multiple_of(c * chunk, chunk), chunk)
        for b in range(bands):
            phi = phi_ref[b, :, px]
            tpl_ref[b, 0:size_k, px] = phi
            tpl_ref[b, size_k : 2 * size_k, px] = psi_ref[b, :, px]
            pair_ref[b, :, px] = (dot(left_ref[...], phi) * dot(right_ref[...], phi)).astype(bf16)
            prow_ref[b, :, px] = dot(grad_ref[...], phi).astype(bf16)
        return carry

    lax.fori_loop(0, pix // chunk, step, 0)


def unfold(ref, rows, lane, i, left):
    x, y = ref[2 * i, rows, :], ref[2 * i + 1, rows, :]
    if left:
        return jnp.where(lane < LANES // 2, x, pltpu.roll(y, LANES // 2, 1))
    return jnp.where(lane < LANES // 2, pltpu.roll(x, LANES // 2, 1), y)


def index_kernel(sizes, got_ref, small_ref, pick_ref, member_ref, theta_ref, table_ref, hot_ref):
    n_sky, cap, obj_dev, nei = sizes
    stamps = small_ref.shape[1]
    total = n_sky * cap
    n_all = n_sky * obj_dev
    lane = iota((8, LANES), 1)
    for d in range(n_sky):
        theta_ref[d] = got_ref[d, 0:8, :]
    for i in range(n_sky // 2):
        span = slice(i * LANES, (i + 1) * LANES)
        table_ref[0:8, span] = unfold(got_ref, slice(8, 16), lane, i, True)
        table_ref[8:16, span] = unfold(got_ref, slice(8, 16), lane, i, False)
    owner = (small_ref[0:1, :] * obj_dev + small_ref[1:2, :]).astype(jnp.int32)
    block = 2 * obj_dev

    def hot(i, carry):
        rows = pl.ds(pl.multiple_of(i * block, block), block)
        hit = iota((block, stamps), 0) + i * block == owner
        hot_ref[rows, :] = jnp.where(hit, 1.0, 0.0).astype(bf16)
        return carry

    lax.fori_loop(0, n_all // block, hot, 0)
    parts = jnp.concatenate(split3(table_ref[...]), axis=0)
    found = dot(parts, hot_ref[...])
    found = found[0:16] + found[16:32] + found[32:48]
    near_id = found[0:nei].astype(jnp.int32)
    near_w = found[8 : 8 + nei]

    def blend(i, carry):
        rows = pl.ds(pl.multiple_of(i * block, block), block)
        here = iota((block, stamps), 0) + i * block
        mix = jnp.zeros((block, stamps), f32)
        for j in range(nei):
            mix = mix + jnp.where(here == near_id[j : j + 1], near_w[j : j + 1], 0.0)
        high = mix.astype(bf16)
        pick_ref[rows, 0:stamps] = hot_ref[rows, :]
        pick_ref[rows, stamps : 2 * stamps] = high
        pick_ref[rows, 2 * stamps : 3 * stamps] = (mix - high.astype(f32)).astype(bf16)
        return carry

    lax.fori_loop(0, n_all // block, blend, 0)
    ids = got_ref[:, 8 + nei, :]
    turn = jnp.where(
        iota((LANES, total), 0) == lax.rem(iota((LANES, total), 1), cap), 1.0, 0.0
    )
    spread = dot(ids, turn, precision=lax.Precision.HIGHEST)
    slot = iota((n_sky, total), 1)
    own = iota((n_sky, total), 0)
    mine = (slot >= own * cap) & (slot < own * cap + cap)
    row = jnp.sum(jnp.where(mine, spread, 0.0), axis=0, keepdims=True).astype(jnp.int32)
    member_ref[...] = jnp.where(iota((obj_dev, total), 0) + 1 == row, 1.0, 0.0).astype(bf16)


def terms_kernel(
    sizes,
    theta_ref,
    pick_ref,
    small_ref,
    inv_ref,
    pix_ref,
    tpl_ref,
    pair_ref,
    prow_ref,
    sel_ref,
    wide_ref,
    out_ref,
    amp_ref,
    acc_ref,
    lit_ref,
):
    n_sky, cap, fold, chunk, extra = sizes
    bands, stamps, pix = pix_ref.shape
    size_k = tpl_ref.shape[1] // 2
    lane = iota((8, LANES), 1)
    for i in range(n_sky // 2):
        span = slice(i * LANES, (i + 1) * LANES)
        amp_ref[0:8, span] = jnp.exp(unfold(theta_ref, slice(None), lane, i, True))
        amp_ref[8:16, span] = jnp.exp(unfold(theta_ref, slice(None), lane, i, False))
    parts = jnp.concatenate(split3(amp_ref[...]), axis=0)
    got = dot(parts, pick_ref[...])
    k1, k2, k3 = slice(0, size_k), slice(size_k, 2 * size_k), slice(2 * size_k, 3 * size_k)
    s1, s2, s3 = slice(0, stamps), slice(stamps, 2 * stamps), slice(2 * stamps, 3 * stamps)
    slot_f = got[k1, s1] + (got[k2, s1] + got[k3, s1])
    slot_u = got[k1, s2] + (got[k2, s2] + got[k1, s3] + (got[k3, s2] + got[k2, s3]))
    scaled = small_ref[2:3, :] * slot_f
    lit_ref[...] = jnp.concatenate([scaled, slot_u], axis=0).T.astype(bf16)
    acc_ref[...] = jnp.zeros_like(acc_ref)
    inv = jnp.concatenate([inv_ref[...]] * (chunk // LANES), axis=1)
    slope = inv * (1.0 / ROBUST)
    wide = pair_ref.shape[1]

    for b in range(bands):

        def step(c, carry):
            px = pl.ds(pl.multiple_of(c * chunk, chunk), chunk)
            model = dot(lit_ref[...], tpl_ref[b, :, px])
            resid = pix_ref[b, :, px].astype(f32) - model
            under = 1.0 + slope * (resid * resid)
            guess = pl.reciprocal(under, approx=True)
            weight = inv * (guess * (2.0 - under * guess))
            low = weight.astype(bf16)
            wres = (weight * resid).astype(bf16)
            acc_ref[:, 0:wide] += dot(low, pair_ref[b, :, px], NT)
            acc_ref[:, LANES : LANES + GROUP] += dot(wres, prow_ref[b, :, px], NT)
            return carry

        lax.fori_loop(0, pix // chunk, step, 0)

    scales = dot(jnp.concatenate(split3(scaled), axis=0), wide_ref[...], TN)
    col = iota((1, 2 * LANES), 1) - (LANES + extra)
    is_grad = jnp.where((col >= 0) & (col < size_k), 1.0, 0.0)
    terms = scales[:, : 2 * LANES] * (scales[:, 2 * LANES :] + is_grad) * acc_ref[...]
    t1, t2, t3 = split3(terms)
    sel = sel_ref[...]
    rows = dot(sel, t1) + (dot(sel, t2) + dot(sel, t3))
    per = cap // fold
    for d in range(n_sky):
        base = d * cap
        out_ref[d, 0:cap, :] = rows[base : base + cap, :LANES]
        tail = rows[base : base + per, LANES:]
        for g in range(1, fold):
            at = base + g * per
            tail = tail + pltpu.roll(rows[at : at + per, LANES:], g * GROUP, 1)
        out_ref[d, cap : cap + per, :] = tail


def solve_kernel(
    sizes,
    recv_ref,
    other_ref,
    member_ref,
    full_ref,
    theta_ref,
    init_ref,
    pay_ref,
    new_ref,
    rows_ref,
):
    n_sky, cap, fold = sizes
    per = cap // fold
    size_k, obj_dev = theta_ref.shape
    group = iota((per, LANES), 1) // GROUP
    for d in range(n_sky):
        both = recv_ref[d] + other_ref[d]
        rows_ref[d * cap : d * cap + cap, 0:LANES] = both[0:cap]
        tail = both[cap : cap + per]
        for g in range(fold):
            at = d * cap + g * per
            rows_ref[at : at + per, LANES:] = jnp.where(group == g, tail, 0.0)
    p1, p2, p3 = split3(rows_ref[...])
    member = member_ref[...]
    sums = dot(member, p1) + (dot(member, p2) + dot(member, p3))
    q1, q2, q3 = split3(sums)
    full = full_ref[...]
    wide = dot(full, q1, NT) + (dot(full, q2, NT) + dot(full, q3, NT))
    row = iota((size_k, obj_dev), 0)
    theta = theta_ref[...]
    target = wide[size_k * size_k :] - PRIOR * (theta - init_ref[...])
    matrix = []
    for k in range(size_k):
        line = wide[k * size_k : (k + 1) * size_k]
        matrix.append(jnp.where(row == k, line + (DAMPING * line + PRIOR), line))
    inverse = []
    for p in range(size_k):
        line = matrix[p]
        inv = 1.0 / line[p : p + 1]
        inverse.append(inv)
        if p + 1 < size_k:
            scaled = jnp.where(row > p, line * inv, 0.0)
            target = target - scaled * target[p : p + 1]
            for k in range(p + 1, size_k):
                matrix[k] = matrix[k] - scaled * line[k : k + 1]
    delta = jnp.zeros_like(target)
    for p in reversed(range(size_k)):
        value = target[p : p + 1] * inverse[p]
        delta = jnp.where(row == p, value, delta)
        if p:
            target = target - matrix[p] * value
    new = theta + STEP_LIMIT * jnp.tanh(delta / STEP_LIMIT)
    new_ref[...] = new
    half = size_k // 2
    folded = jnp.concatenate([new[:half], new[half:]], axis=1)
    for d in range(n_sky):
        pay_ref[d] = folded


def call(kernel, out_shape, scratch=()):
    return pl.pallas_call(
        kernel,
        out_shape=out_shape,
        scratch_shapes=list(scratch),
        compiler_params=pltpu.CompilerParams(vmem_limit_bytes=VMEM_LIMIT),
    )


def local(
    stamps,
    stamp_gain,
    stamp_invvar,
    stamp_dest,
    stamp_obj,
    phi_tpl,
    psi_tpl,
    theta_init,
    nb_id,
    nb_weight,
):
    n_sky = lax.axis_size("sky")
    n_band = lax.axis_size("band")
    stamp_dev, bands, pix = stamps.shape
    size_k, obj_dev = theta_init.shape
    nei = nb_id.shape[1]
    cap = 2 * stamp_dev // n_sky
    fold = max(1, min(LANES // GROUP, cap // 8))
    total = n_sky * cap
    n_all = n_sky * obj_dev
    rows = cap + cap // fold
    left, right, grad, full = tables(size_k)
    extra = size_k * (size_k + 1) // 2 - LANES
    wide = LANES + GROUP
    shape = jax.ShapeDtypeStruct

    pixels = jnp.transpose(stamps, (1, 0, 2))
    small = jnp.stack(
        [
            stamp_dest[:, 0].astype(f32),
            stamp_obj.astype(f32),
            stamp_gain.astype(f32),
            stamp_invvar.astype(f32),
        ]
    )
    payload, sel, inv = call(
        functools.partial(first_kernel, (n_sky, cap, obj_dev)),
        (
            shape((n_sky, 16, LANES), f32),
            shape((total, stamp_dev), bf16),
            shape((stamp_dev, LANES), f32),
        ),
    )(small, theta_init, nb_id.T, nb_weight.T)
    got = lax.all_to_all(payload, "sky", 0, 0, tiled=True)
    tpl, pair, prow = call(
        pair_kernel,
        (
            shape((bands, 2 * size_k, pix), bf16),
            shape((bands, wide, pix), bf16),
            shape((bands, GROUP, pix), bf16),
        ),
    )(
        phi_tpl,
        psi_tpl,
        jnp.asarray(left.T[:wide], bf16),
        jnp.asarray(right.T[:wide], bf16),
        jnp.asarray(grad.T[LANES:wide], bf16),
    )
    pick, member, everyone = call(
        functools.partial(index_kernel, (n_sky, cap, obj_dev, nei)),
        (
            shape((n_all, 3 * stamp_dev), bf16),
            shape((obj_dev, total), bf16),
            shape((n_sky, 8, LANES), f32),
        ),
        [pltpu.VMEM((16, n_all), f32), pltpu.VMEM((n_all, stamp_dev), bf16)],
    )(got, small)
    spread = np.concatenate([np.concatenate([left + grad, right], axis=1)] * 3, axis=0)
    terms = call(
        functools.partial(terms_kernel, (n_sky, cap, fold, 256, extra)),
        shape((n_sky, rows, LANES), f32),
        [
            pltpu.VMEM((size_k, n_all), f32),
            pltpu.VMEM((stamp_dev, 2 * LANES), f32),
            pltpu.VMEM((stamp_dev, 2 * size_k), bf16),
        ],
    )
    solve = call(
        functools.partial(solve_kernel, (n_sky, cap, fold)),
        (shape((n_sky, 8, LANES), f32), shape((size_k, obj_dev), f32)),
        [pltpu.VMEM((total, 2 * LANES), f32)],
    )
    spread = jnp.asarray(spread, bf16)
    full = jnp.asarray(full, bf16)
    theta = theta_init
    for sweep in range(ITERS):
        sent = terms(everyone, pick, small, inv, pixels, tpl, pair, prow, sel, spread)
        recv = lax.all_to_all(sent, "sky", 0, 0, tiled=True)
        if n_band == 2:
            other = lax.ppermute(recv, "band", [(0, 1), (1, 0)])
        else:
            other = lax.psum(recv, "band") - recv
        payload, theta = solve(recv, other, member, full, theta, theta_init)
        if sweep + 1 < ITERS:
            everyone = lax.all_to_all(payload, "sky", 0, 0, tiled=True)
    return theta


def solution(mesh):
    in_specs = (
        P("sky", "band", None),
        P("sky"),
        P("sky"),
        P("sky", None),
        P("sky"),
        P("band", None, None),
        P("band", None, None),
        P(None, "sky"),
        P("sky", None),
        P("sky", None),
    )
    out_specs = P(None, "sky")
    return jax.shard_map(local, mesh=mesh, in_specs=in_specs, out_specs=out_specs, check_vma=False)
```

profile of v0, /device:TPU:0, one launch (start us, length us, event | category | flops | bytes accessed | tf_op | source)
XLA Modules:
  0.0 136.5 jit_solution(1799332600131628551)
XLA Ops:
  4.8 1.6 %shard_map.145 = (f32[16,16,128]{2,1,0:T(8,128)}, bf16[512,256]{1,0:T(8,128)(2,1)S(1)}, f32[256,128]{1,0:T(8,128)S(1)}) custom-call(f32[4,256]{1,0:T(4,128)S(1)} %pad_maximum_fusion.small_ref, f32[16,64]{1,0:T(8,128)S(1)} %copy-done.7, s32[4,64]{1,0:T(4,128)S(1)} %bitcast.11, f32[4,64]{1,0:T(4,128)S(1)} %bitcast.12), custom_call_target="tpu_custom_call" | custom-call | tf_op jit(solution)/shard_map/pallas_call | solution.py:358
  6.3 8.4 %all-to-all-start = ((f32[16,16,128]{2,1,0:T(8,128)}), f32[16,16,128]{2,1,0:T(8,128)}, u32[]{:S(2)}, u32[]{:S(2)}) async-start(f32[16,16,128]{2,1,0:T(8,128)} %get-tuple-element.19), calls=%async_computation | async-start | bytes 262144 | tf_op jit(solution)/shard_map/all_to_all | solution.py:366
  14.7 0.9 copy-done.5
  15.7 0.9 copy-done.6
  16.6 0.8 copy-done.9
  18.8 2.4 %shard_map.147 = (bf16[3,32,2304]{2,1,0:T(8,128)(2,1)S(1)}, bf16[3,160,2304]{2,1,0:T(8,128)(2,1)S(1)}, bf16[3,32,2304]{2,1,0:T(8,128)(2,1)S(1)}) custom-call(bf16[3,16,2304]{2,1,0:T(8,128)(2,1)S(1)} %copy-done.5, bf16[3,16,2304]{2,1,0:T(8,128)(2,1)S(1)} %copy-done.6, bf16[160,16]{1,0:T(8,128)(2,1)S(1)} %copy-done.10, bf16[160,16]{1,0:T(8,128)(2,1)S(1)} %copy-done.9, ...), custom_call_target="tpu_custom_call" | custom-call | tf_op jit(solution)/shard_map/pallas_call | solution.py:367
  21.3 1.3 all-to-all-done.got_ref
  22.6 2.2 %shard_map.146 = (bf16[1024,768]{1,0:T(8,128)(2,1)S(1)}, bf16[64,512]{1,0:T(8,128)(2,1)S(1)}, f32[16,8,128]{2,1,0:T(8,128)S(1)}) custom-call(f32[16,16,128]{2,1,0:T(8,128)} %all-to-all-done.got_ref, f32[4,256]{1,0:T(4,128)S(1)} %pad_maximum_fusion.small_ref), custom_call_target="tpu_custom_call" | custom-call | tf_op jit(solution)/shard_map/pallas_call | solution.py:381
  24.7 2.0 %copy-done = bf16[256,3,2304]{2,0,1:T(8,128)(2,1)S(1)} copy-done((bf16[256,3,2304]{2,0,1:T(8,128)(2,1)S(1)}, bf16[256,3,2304]{2,0,1:T(8,128)(2,1)}, u32[]{:S(2)}) %copy-start) | copy-done | bytes 3538968
  26.7 0.8 copy-done.3
  27.5 12.1 %shard_map.148 = f32[16,40,128]{2,1,0:T(8,128)S(1)} custom-call(f32[16,8,128]{2,1,0:T(8,128)S(1)} %get-tuple-element.20.theta_ref, bf16[1024,768]{1,0:T(8,128)(2,1)S(1)} %get-tuple-element.21.pick_ref, f32[4,256]{1,0:T(4,128)S(1)} %pad_maximum_fusion.small_ref, f32[256,128]{1,0:T(8,128)S(1)} %get-tuple-element.22.inv_ref, bf16[3,256,2304]{2,1,0:T(8,128)(2,1)S(1)} %bitcast.8, ...), custom_call_target="tpu_custom_call" | custom-call | tf_op jit(solution)/shard_map/pallas_call | solution.py:409
  39.7 16.2 %all_to_all.30.recv_ref = f32[16,40,128]{2,1,0:T(8,128)S(1)} all-to-all(f32[16,40,128]{2,1,0:T(8,128)S(1)} %shard_map.148), channel_id=1, replica_groups=mesh['sky'=16,'band'=2] {'sky'}, dimensions={0} | all-to-all | bytes 655360 | tf_op jit(solution)/shard_map/all_to_all | solution.py:410
  55.9 1.6 %collective-permute-done.other_ref = f32[16,40,128]{2,1,0:T(8,128)S(1)} collective-permute-done((f32[16,40,128]{2,1,0:T(8,128)S(1)}, f32[16,40,128]{2,1,0:T(8,128)S(1)}, u32[]{:S(2)}, u32[]{:S(2)}) %collective-permute-start) | collective-permute-done | bytes 327712 | tf_op jit(solution)/shard_map/ppermute | solution.py:412
  57.5 0.9 shard_map.149
  58.4 10.8 %all_to_all.31.theta_ref = f32[16,8,128]{2,1,0:T(8,128)S(1)} all-to-all(f32[16,8,128]{2,1,0:T(8,128)S(1)} %get-tuple-element.28), channel_id=1, replica_groups=mesh['sky'=16,'band'=2] {'sky'}, dimensions={0} | all-to-all | bytes 131072 | tf_op jit(solution)/shard_map/all_to_all | solution.py:417
  69.3 12.1 %shard_map.150 = f32[16,40,128]{2,1,0:T(8,128)S(1)} custom-call(f32[16,8,128]{2,1,0:T(8,128)S(1)} %all_to_all.31.theta_ref, bf16[1024,768]{1,0:T(8,128)(2,1)S(1)} %get-tuple-element.21.pick_ref, f32[4,256]{1,0:T(4,128)S(1)} %pad_maximum_fusion.small_ref, f32[256,128]{1,0:T(8,128)S(1)} %get-tuple-element.22.inv_ref, bf16[3,256,2304]{2,1,0:T(8,128)(2,1)S(1)} %bitcast.9, ...), custom_call_target="tpu_custom_call" | custom-call | tf_op jit(solution)/shard_map/pallas_call | solution.py:409
  81.4 13.2 %all_to_all.32.recv_ref = f32[16,40,128]{2,1,0:T(8,128)S(1)} all-to-all(f32[16,40,128]{2,1,0:T(8,128)S(1)} %shard_map.150), channel_id=1, replica_groups=mesh['sky'=16,'band'=2] {'sky'}, dimensions={0} | all-to-all | bytes 655360 | tf_op jit(solution)/shard_map/all_to_all | solution.py:410
  94.6 1.6 %collective-permute-done.1.other_ref = f32[16,40,128]{2,1,0:T(8,128)S(1)} collective-permute-done((f32[16,40,128]{2,1,0:T(8,128)S(1)}, f32[16,40,128]{2,1,0:T(8,128)S(1)}, u32[]{:S(2)}, u32[]{:S(2)}) %collective-permute-start.1) | collective-permute-done | bytes 327712 | tf_op jit(solution)/shard_map/ppermute | solution.py:412
  96.2 0.9 shard_map.151
  97.1 10.8 %all_to_all.33.theta_ref = f32[16,8,128]{2,1,0:T(8,128)S(1)} all-to-all(f32[16,8,128]{2,1,0:T(8,128)S(1)} %get-tuple-element.30), channel_id=1, replica_groups=mesh['sky'=16,'band'=2] {'sky'}, dimensions={0} | all-to-all | bytes 131072 | tf_op jit(solution)/shard_map/all_to_all | solution.py:417
  108.0 12.1 %shard_map.152 = f32[16,40,128]{2,1,0:T(8,128)S(1)} custom-call(f32[16,8,128]{2,1,0:T(8,128)S(1)} %all_to_all.33.theta_ref, bf16[1024,768]{1,0:T(8,128)(2,1)S(1)} %get-tuple-element.21.pick_ref, f32[4,256]{1,0:T(4,128)S(1)} %pad_maximum_fusion.small_ref, f32[256,128]{1,0:T(8,128)S(1)} %get-tuple-element.22.inv_ref, bf16[3,256,2304]{2,1,0:T(8,128)(2,1)S(1)} %bitcast.10, ...), custom_call_target="tpu_custom_call" | custom-call | tf_op jit(solution)/shard_map/pallas_call | solution.py:409
  120.1 13.2 %all_to_all.34.recv_ref = f32[16,40,128]{2,1,0:T(8,128)S(1)} all-to-all(f32[16,40,128]{2,1,0:T(8,128)S(1)} %shard_map.152), channel_id=1, replica_groups=mesh['sky'=16,'band'=2] {'sky'}, dimensions={0} | all-to-all | bytes 655360 | tf_op jit(solution)/shard_map/all_to_all | solution.py:410
  133.2 1.6 %collective-permute-done.2.other_ref = f32[16,40,128]{2,1,0:T(8,128)S(1)} collective-permute-done((f32[16,40,128]{2,1,0:T(8,128)S(1)}, f32[16,40,128]{2,1,0:T(8,128)S(1)}, u32[]{:S(2)}, u32[]{:S(2)}) %collective-permute-start.2) | collective-permute-done | bytes 327712 | tf_op jit(solution)/shard_map/ppermute | solution.py:412
  134.9 1.6 %shard_map.153 = (f32[16,8,128]{2,1,0:T(8,128)}, f32[16,64]{1,0:T(8,128)}) custom-call(f32[16,40,128]{2,1,0:T(8,128)S(1)} %all_to_all.34.recv_ref, f32[16,40,128]{2,1,0:T(8,128)S(1)} %collective-permute-done.2.other_ref, bf16[64,512]{1,0:T(8,128)(2,1)S(1)} %get-tuple-element.27.member_ref, bf16[272,256]{1,0:T(8,128)(2,1)S(1)} %copy-done.2, ...), custom_call_target="tpu_custom_call" | custom-call | tf_op jit(solution)/shard_map/pallas_call | solution.py:415
  (31 shorter events, 6.3 us)
Async XLA Ops:
  2.7 0.7 copy-start.7
  3.4 0.7 copy-start.12
  4.1 0.7 copy-start.13
  6.3 16.2 %all-to-all-start = ((f32[16,16,128]{2,1,0:T(8,128)}), f32[16,16,128]{2,1,0:T(8,128)}, u32[]{:S(2)}, u32[]{:S(2)}) async-start(f32[16,16,128]{2,1,0:T(8,128)} %get-tuple-element.19), calls=%async_computation | async-start | bytes 262144 | tf_op jit(solution)/shard_map/all_to_all | solution.py:366
  14.7 0.9 copy-start.5
  15.7 0.9 copy-start.6
  16.6 0.8 copy-start.9
  17.4 0.8 copy-start.10
  18.1 0.7 copy-start.11
  24.7 2.0 %copy-start = (bf16[256,3,2304]{2,0,1:T(8,128)(2,1)S(1)}, bf16[256,3,2304]{2,0,1:T(8,128)(2,1)}, u32[]{:S(2)}) copy-start(bf16[256,3,2304]{2,0,1:T(8,128)(2,1)} %param.15) | copy-start | bytes 10616836
  26.7 0.8 copy-start.3
  27.5 29.9 %copy-start.2 = (bf16[272,256]{1,0:T(8,128)(2,1)S(1)}, bf16[272,256]{1,0:T(8,128)(2,1)}, u32[]{:S(2)}) copy-start(bf16[272,256]{1,0:T(8,128)(2,1)} %constant.14.clone.full_ref) | copy-start | bytes 417796
  27.5 29.9 %copy-start.8 = (f32[16,64]{1,0:T(8,128)S(1)}, f32[16,64]{1,0:T(8,128)}, u32[]{:S(2)}) copy-start(f32[16,64]{1,0:T(8,128)} %init_ref.5) | copy-start | bytes 12292
  27.5 41.7 %copy-start.1 = (bf16[256,3,2304]{2,0,1:T(8,128)(2,1)S(1)}, bf16[256,3,2304]{2,0,1:T(8,128)(2,1)}, u32[]{:S(2)}) copy-start(bf16[256,3,2304]{2,0,1:T(8,128)(2,1)} %param.15) | copy-start | bytes 10616836
  27.5 41.7 %copy-start.4 = (bf16[48,512]{1,0:T(8,128)(2,1)S(1)}, bf16[48,512]{1,0:T(8,128)(2,1)}, u32[]{:S(2)}) copy-start(bf16[48,512]{1,0:T(8,128)(2,1)} %constant.13.clone.wide_ref) | copy-start | bytes 147460
  55.8 1.6 %collective-permute-start = (f32[16,40,128]{2,1,0:T(8,128)S(1)}, f32[16,40,128]{2,1,0:T(8,128)S(1)}, u32[]{:S(2)}, u32[]{:S(2)}) collective-permute-start(f32[16,40,128]{2,1,0:T(8,128)S(1)} %all_to_all.30.recv_ref), channel_id=1, source_target_pairs={{0,1},{1,0},{2,3},{3,2},{4,5},{5,4},{6,7},{7,6},{8,9},{9,8},{10,11... | collective-permute-start | bytes 983048 | tf_op jit(solution)/shard_map/ppermute | solution.py:412
  94.6 1.6 %collective-permute-start.1 = (f32[16,40,128]{2,1,0:T(8,128)S(1)}, f32[16,40,128]{2,1,0:T(8,128)S(1)}, u32[]{:S(2)}, u32[]{:S(2)}) collective-permute-start(f32[16,40,128]{2,1,0:T(8,128)S(1)} %all_to_all.32.recv_ref), channel_id=1, source_target_pairs={{0,1},{1,0},{2,3},{3,2},{4,5},{5,4},{6,7},{7,6},{8,9},{9,8},{10,11... | collective-permute-start | bytes 983048 | tf_op jit(solution)/shard_map/ppermute | solution.py:412
  133.2 1.6 %collective-permute-start.2 = (f32[16,40,128]{2,1,0:T(8,128)S(1)}, f32[16,40,128]{2,1,0:T(8,128)S(1)}, u32[]{:S(2)}, u32[]{:S(2)}) collective-permute-start(f32[16,40,128]{2,1,0:T(8,128)S(1)} %all_to_all.34.recv_ref), channel_id=1, source_target_pairs={{0,1},{1,0},{2,3},{3,2},{4,5},{5,4},{6,7},{7,6},{8,9},{9,8},{10,11... | collective-permute-start | bytes 983048 | tf_op jit(solution)/shard_map/ppermute | solution.py:412
where the time goes:
time: 137 us; the launch traced here: 136 us
  blocking collectives  64.1 us (47%)
  Pallas kernels  46 us (34%)
  local copies, waits for them, and re-layouts  8.98 us (7%)
  starting transfers between devices  8.4 us (6%)
  waiting for transfers between devices  6.16 us (4%)
  other arithmetic  2.69 us (2%)
    all_to_all x3, blocking collectives, local(): recv = lax.all_to_all(sent, 'sky', 0, 0, tiled=True)  42.5 us
    pallas_call x3, Pallas kernels, local(): terms(everyone, pick, small, inv, pixels, tpl, pair, prow, sel, spread)  36.4 us
    all_to_all x2, blocking collectives, local(): everyone = lax.all_to_all(payload, 'sky', 0, 0, tiled=True)  21.6 us
    unnamed x28, local copies, waits for them, and re-layouts  8.98 us
    all_to_all x1, starting transfers between devices, local(): got = lax.all_to_all(payload, 'sky', 0, 0, tiled=True)  8.39 us
    ppermute x3, waiting for transfers between devices, local(): other = lax.ppermute(recv, 'band', [(0, 1), (1, 0)])  4.88 us
    pallas_call x3, Pallas kernels, local(): payload, theta = solve(recv, other, member, full, theta, theta_init)  3.48 us
  transfers between devices with their start and end apart: 4, of which 4 were waited for; matrix products, arithmetic and copies ran while one was open for 0% of the time, Pallas kernels for 2%

commit v1 on v0

v1 whole, which is shorter than its diff:
```python
import functools

import jax
import jax.numpy as jnp
from jax import lax
from jax.experimental import pallas as pl
from jax.experimental.pallas import tpu as pltpu
from jax.sharding import PartitionSpec as P

ITERS = 3

ROBUST = 9.0
DAMPING = 0.1
PRIOR = 1.0
STEP_LIMIT = 0.5

LANES = 128
GROUP = 32
VMEM_LIMIT = 24 * 1024 * 1024

f32 = jnp.float32
bf16 = jnp.bfloat16
NT = (((1,), (1,)), ((), ()))
TN = (((0,), (0,)), ((), ()))
NN = (((1,), (0,)), ((), ()))


def dot(a, b, dims=NN, precision=None):
    return lax.dot_general(a, b, dims, precision=precision, preferred_element_type=f32)


def split3(x):
    first = x.astype(bf16)
    rest = x - first.astype(f32)
    second = rest.astype(bf16)
    third = (rest - second.astype(f32)).astype(bf16)
    return first, second, third


def iota(shape, dim):
    return lax.broadcasted_iota(jnp.int32, shape, dim)


def dma(copies):
    for copy in copies:
        copy.start()
    return copies


def wait(copies):
    for copy in copies:
        copy.wait()


def offset(k, size_k):
    return lax.div(k * (2 * size_k + 1 - k), 2)


def column(shape, m):
    lane = iota(shape, 1)
    folded = jnp.where(lane < LANES, lane, LANES + lax.rem(lane, GROUP))
    return folded == m


def pack_kernel(theta_hbm, nbi_hbm, nbw_hbm, pay_ref, theta_ref, nbi_ref, nbw_ref, sem):
    n_sky = pay_ref.shape[0]
    wait(
        dma(
            [
                pltpu.make_async_copy(theta_hbm, theta_ref, sem.at[0]),
                pltpu.make_async_copy(nbi_hbm, nbi_ref, sem.at[1]),
                pltpu.make_async_copy(nbw_hbm, nbw_ref, sem.at[2]),
            ]
        )
    )
    half = theta_ref.shape[0] // 2
    theta = theta_ref[...]
    folded = jnp.concatenate([theta[:half], theta[half:]], axis=1)
    side = jnp.concatenate([nbi_ref[...].astype(f32), nbw_ref[...]], axis=1)
    side = jnp.concatenate([side, jnp.zeros((8 - side.shape[0], LANES), f32)], axis=0)
    for d in range(n_sky):
        pay_ref[d, 0:8, :] = folded
        pay_ref[d, 8:16, :] = side


def ready_kernel(
    sizes,
    dest_hbm,
    obj_hbm,
    gain_hbm,
    invvar_hbm,
    phi_hbm,
    psi_hbm,
    tpl_ref,
    pair_ref,
    sel_ref,
    wide_ref,
    full_ref,
    base_ref,
    tag_ref,
    gain_ref,
    owner_ref,
    dest_ref,
    obj_ref,
    gain_low_ref,
    invvar_ref,
    sem,
):
    n_sky, cap, obj_dev, extra = sizes
    bands, size_k, pix = phi_hbm.shape
    stamps = dest_ref.shape[1]
    total = n_sky * cap
    first = [
        pltpu.make_async_copy(phi_hbm, tpl_ref.at[:, 0:size_k, :], sem.at[0]),
        pltpu.make_async_copy(psi_hbm, tpl_ref.at[:, size_k : 2 * size_k, :], sem.at[1]),
        pltpu.make_async_copy(dest_hbm, dest_ref, sem.at[2]),
        pltpu.make_async_copy(obj_hbm, obj_ref, sem.at[3]),
        pltpu.make_async_copy(gain_hbm, gain_low_ref, sem.at[4]),
        pltpu.make_async_copy(invvar_hbm, invvar_ref, sem.at[5]),
    ]
    dma(first)

    pairs = LANES + extra
    shape = (pair_ref.shape[1], size_k)
    m = iota(shape, 0)
    k = iota(shape, 1)
    lows = jnp.where((m >= offset(k, size_k)) & (m < offset(k + 1, size_k)), 1.0, 0.0)
    of_m = jnp.sum(lows * k.astype(f32), axis=1, keepdims=True).astype(jnp.int32)
    highs = jnp.where((m < pairs) & (m - offset(of_m, size_k) + of_m == k), 1.0, 0.0)
    lows, highs = lows.astype(bf16), highs.astype(bf16)

    shape = (size_k, 2 * LANES)
    k = iota(shape, 0)
    lane = iota(shape, 1)
    spot = pairs + k
    left = (lane >= offset(k, size_k)) & (lane < offset(k + 1, size_k))
    left = jnp.where(left | (lane == spot), 1.0, 0.0)
    lane_k = jnp.sum(jnp.where(lane >= offset(k + 1, size_k), 1, 0), axis=0, keepdims=True)
    right = (lane[0:1] - offset(lane_k, size_k) + lane_k == k) & (lane < pairs)
    both = jnp.concatenate([left, jnp.where(right, 1.0, 0.0)], axis=1).astype(bf16)
    for part in range(3):
        wide_ref[part * size_k : (part + 1) * size_k, :] = both

    shape = full_ref.shape
    r = iota((shape[0], 1), 0)
    a, b = lax.div(r, size_k), lax.rem(r, size_k)
    low, high = jnp.minimum(a, b), jnp.maximum(a, b)
    m = jnp.where(r < size_k * size_k, offset(low, size_k) + high - low, pairs + b)
    full_ref[...] = jnp.where(column(shape, m), 1.0, 0.0).astype(bf16)

    wait(first)
    dest = dest_ref[...]
    obj = obj_ref[...]
    gain_ref[...] = jnp.broadcast_to(gain_low_ref[...].astype(f32), gain_ref.shape)
    base_ref[...] = jnp.broadcast_to(1.0 / invvar_ref[...].astype(f32), (LANES, stamps)).T
    named = jnp.broadcast_to((obj + 1).astype(f32), (LANES, stamps)).T
    tag_ref[...] = jnp.where(
        iota((stamps, LANES), 1) == extra + size_k, named, 0.0
    )
    along = jnp.broadcast_to(dest.astype(f32), (stamps, stamps))
    before = iota((stamps, stamps), 0) < iota((stamps, stamps), 1)
    rank = jnp.sum(jnp.where(before & (along == along.T), 1.0, 0.0), axis=0, keepdims=True)
    owner_ref[...] = jnp.broadcast_to(dest * obj_dev + obj, owner_ref.shape)
    place = dest * cap + rank.astype(jnp.int32)
    sel_ref[...] = jnp.where(iota((total, stamps), 0) == place, 1.0, 0.0).astype(bf16)
    chunk = 256

    def step(c, carry):
        px = pl.ds(pl.multiple_of(c * chunk, chunk), chunk)
        for b in range(bands):
            phi = tpl_ref[b, 0:size_k, px]
            pair_ref[b, :, px] = (dot(lows, phi) * dot(highs, phi)).astype(bf16)
        return carry

    lax.fori_loop(0, pix // chunk, step, 0)


def unfold(ref, rows, lane, i, left):
    x, y = ref[2 * i, rows, :], ref[2 * i + 1, rows, :]
    if left:
        return jnp.where(lane < LANES // 2, x, pltpu.roll(y, LANES // 2, 1))
    return jnp.where(lane < LANES // 2, pltpu.roll(x, LANES // 2, 1), y)


def index_kernel(nei, got_ref, owner_ref, theta_ref, hot_ref, blend_ref, table_ref):
    n_sky = got_ref.shape[0]
    n_all, stamps = hot_ref.shape
    block = LANES
    owner = owner_ref[0:1, :]

    def hot(i, carry):
        rows = pl.ds(pl.multiple_of(i * block, block), block)
        hit = iota((block, stamps), 0) + i * block == owner
        hot_ref[rows, :] = jnp.where(hit, 1.0, 0.0).astype(bf16)
        return carry

    lax.fori_loop(0, n_all // block, hot, 0)
    lane = iota((8, LANES), 1)
    for d in range(n_sky):
        theta_ref[d] = got_ref[d, 0:8, :]
    for i in range(n_sky // 2):
        span = slice(i * LANES, (i + 1) * LANES)
        table_ref[0:8, span] = unfold(got_ref, slice(8, 16), lane, i, True)
        table_ref[8:16, span] = unfold(got_ref, slice(8, 16), lane, i, False)
    parts = jnp.concatenate(split3(table_ref[...]), axis=0)
    found = dot(parts, hot_ref[...])
    found = found[0:16] + found[16:32] + found[32:48]
    near_id = found[0:nei].astype(jnp.int32)
    near_w = found[8 : 8 + nei]

    def blend(i, carry):
        rows = pl.ds(pl.multiple_of(i * block, block), block)
        here = iota((block, stamps), 0) + i * block
        mix = jnp.zeros((block, stamps), f32)
        for j in range(nei):
            mix = mix + jnp.where(here == near_id[j : j + 1], near_w[j : j + 1], 0.0)
        high = mix.astype(bf16)
        blend_ref[rows, 0:stamps] = high
        blend_ref[rows, stamps : 2 * stamps] = (mix - high.astype(f32)).astype(bf16)
        return carry

    lax.fori_loop(0, n_all // block, blend, 0)


def terms_kernel(
    sizes,
    theta_ref,
    hot_ref,
    blend_ref,
    gain_ref,
    base_ref,
    tag_ref,
    pix_hbm,
    tpl_ref,
    pair_ref,
    sel_ref,
    wide_ref,
    out_ref,
    amp_ref,
    acc_ref,
    proj_ref,
    lit_ref,
    pix_ref,
    sem,
):
    n_sky, cap, fold, chunk, extra = sizes
    bands, stamps, pix = pix_ref.shape
    size_k = tpl_ref.shape[1] // 2
    steps = [
        (b, slice(c * chunk, (c + 1) * chunk)) for b in range(bands) for c in range(pix // chunk)
    ]
    loads = dma(
        [
            pltpu.make_async_copy(pix_hbm.at[b, :, px], pix_ref.at[b, :, px], sem.at[i])
            for i, (b, px) in enumerate(steps)
        ]
    )
    lane = iota((8, LANES), 1)
    for i in range(n_sky // 2):
        span = slice(i * LANES, (i + 1) * LANES)
        amp_ref[0:8, span] = jnp.exp(unfold(theta_ref, slice(None), lane, i, True))
        amp_ref[8:16, span] = jnp.exp(unfold(theta_ref, slice(None), lane, i, False))
    parts = jnp.concatenate(split3(amp_ref[...]), axis=0)
    got = dot(parts, hot_ref[...])
    mix = dot(parts, blend_ref[...])
    k1, k2, k3 = slice(0, size_k), slice(size_k, 2 * size_k), slice(2 * size_k, 3 * size_k)
    slot_f = got[k1] + (got[k2] + got[k3])
    high, low = mix[:, :stamps], mix[:, stamps:]
    slot_u = high[k1] + (high[k2] + low[k1] + (high[k3] + low[k2]))
    scaled = gain_ref[0:1, :] * slot_f
    lit_ref[...] = jnp.concatenate([scaled, slot_u], axis=0).T.astype(bf16)
    acc_ref[...] = jnp.zeros_like(acc_ref)
    proj_ref[...] = jnp.zeros_like(proj_ref)
    lit = lit_ref[...]
    base = jnp.concatenate([base_ref[...]] * (chunk // LANES), axis=1)
    wide = pair_ref.shape[1]

    def model(b, px):
        return dot(lit, tpl_ref[b, :, px])

    def weigh(b, px, light):
        resid = pix_ref[b, :, px].astype(f32) - light
        under = base + (resid * resid) * (1.0 / ROBUST)
        guess = pltpu.reciprocal(under, approx=True)
        weight = guess * (2.0 - under * guess)
        return weight.astype(bf16), (weight * resid).astype(bf16)

    def gather(b, px, weight, wres):
        acc_ref[:, 0:wide] += dot(weight, pair_ref[b, :, px], NT)
        proj_ref[:, 0:size_k] += dot(wres, tpl_ref[b, 0:size_k, px], NT)

    light = model(*steps[0])
    held = None
    for i, here in enumerate(steps):
        ahead = model(*steps[i + 1]) if i + 1 < len(steps) else None
        loads[i].wait()
        now = weigh(*here, light)
        if held is not None:
            gather(*steps[i - 1], *held)
        light, held = ahead, now
    gather(*steps[-1], *held)

    scales = dot(jnp.concatenate(split3(scaled), axis=0), wide_ref[...], TN)
    col = iota((1, 2 * LANES), 1) - (LANES + extra)
    is_grad = jnp.where((col >= 0) & (col < size_k), 1.0, 0.0)
    factor = scales[:, : 2 * LANES] * (scales[:, 2 * LANES :] + is_grad)
    tail = acc_ref[:, LANES:] + pltpu.roll(proj_ref[...], extra, 1)
    terms = jnp.concatenate(
        [
            factor[:, :LANES] * acc_ref[:, :LANES],
            factor[:, LANES:] * tail + tag_ref[...],
        ],
        axis=1,
    )
    t1, t2, t3 = split3(terms)
    sel = sel_ref[...]
    rows = dot(sel, t1) + (dot(sel, t2) + dot(sel, t3))
    per = cap // fold
    for d in range(n_sky):
        base_row = d * cap
        out_ref[d, 0:cap, :] = rows[base_row : base_row + cap, :LANES]
        tail = rows[base_row : base_row + per, LANES:]
        for g in range(1, fold):
            at = base_row + g * per
            tail = tail + pltpu.roll(rows[at : at + per, LANES:], g * GROUP, 1)
        out_ref[d, cap : cap + per, :] = tail


def solve_kernel(
    sizes,
    recv_ref,
    other_ref,
    member_in_ref,
    full_ref,
    theta_ref,
    init_ref,
    pay_ref,
    new_ref,
    member_ref,
    rows_ref,
):
    n_sky, cap, fold, n_band, tag, learn = sizes
    per = cap // fold
    size_k, obj_dev = theta_ref.shape
    total = n_sky * cap
    group = iota((per, LANES), 1) // GROUP
    for d in range(n_sky):
        both = recv_ref[d] + other_ref[d]
        rows_ref[d * cap : d * cap + cap, 0:LANES] = both[0:cap]
        tail = both[cap : cap + per]
        for g in range(fold):
            at = d * cap + g * per
            rows_ref[at : at + per, LANES:] = jnp.where(group == g, tail, 0.0)
    p1, p2, p3 = split3(rows_ref[...])
    if learn:
        where_tag = jnp.where(column((8, 2 * LANES), LANES + tag), 1.0, 0.0).astype(bf16)
        ids = dot(where_tag, p1, NT) + (dot(where_tag, p2, NT) + dot(where_tag, p3, NT))
        named = (iota((obj_dev, total), 0) + 1) * n_band
        hit = named == ids[0:1, :].astype(jnp.int32)
        member_ref[...] = jnp.where(hit, 1.0, 0.0).astype(bf16)
        member = member_ref[...]
    else:
        member = member_in_ref[...]
    sums = dot(member, p1) + (dot(member, p2) + dot(member, p3))
    q1, q2, q3 = split3(sums)
    full = full_ref[...]
    wide = dot(full, q1, NT) + (dot(full, q2, NT) + dot(full, q3, NT))
    row = iota((size_k, obj_dev), 0)
    theta = theta_ref[...]
    target = wide[size_k * size_k :] - PRIOR * (theta - init_ref[...])
    matrix = []
    for k in range(size_k):
        line = wide[k * size_k : (k + 1) * size_k]
        matrix.append(jnp.where(row == k, line + (DAMPING * line + PRIOR), line))
    inverse = []
    for p in range(size_k):
        line = matrix[p]
        inv = 1.0 / line[p : p + 1]
        inverse.append(inv)
        if p + 1 < size_k:
            scaled = jnp.where(row > p, line * inv, 0.0)
            target = target - scaled * target[p : p + 1]
            for k in range(p + 1, size_k):
                matrix[k] = matrix[k] - scaled * line[k : k + 1]
    delta = jnp.zeros_like(target)
    for p in reversed(range(size_k)):
        value = target[p : p + 1] * inverse[p]
        delta = jnp.where(row == p, value, delta)
        if p:
            target = target - matrix[p] * value
    new = theta + STEP_LIMIT * jnp.tanh(delta / STEP_LIMIT)
    new_ref[...] = new
    if pay_ref is not None:
        half = size_k // 2
        folded = jnp.concatenate([new[:half], new[half:]], axis=1)
        for d in range(n_sky):
            pay_ref[d] = folded


def hbm(x):
    return pltpu.with_memory_space_constraint(x, pltpu.HBM)


def call(kernel, out_shape, scratch=(), spaces=None):
    specs = {}
    if spaces:
        specs["in_specs"] = [
            pl.BlockSpec(memory_space=pltpu.HBM if s == "h" else pltpu.VMEM) for s in spaces
        ]
    return pl.pallas_call(
        kernel,
        out_shape=out_shape,
        scratch_shapes=list(scratch),
        compiler_params=pltpu.CompilerParams(vmem_limit_bytes=VMEM_LIMIT),
        **specs,
    )


def local(
    stamps,
    stamp_gain,
    stamp_invvar,
    stamp_dest,
    stamp_obj,
    phi_tpl,
    psi_tpl,
    theta_init,
    nb_id,
    nb_weight,
):
    n_sky = lax.axis_size("sky")
    n_band = lax.axis_size("band")
    stamp_dev, bands, pix = stamps.shape
    size_k, obj_dev = theta_init.shape
    nei = nb_id.shape[1]
    cap = 2 * stamp_dev // n_sky
    fold = max(1, min(LANES // GROUP, cap // 8))
    total = n_sky * cap
    n_all = n_sky * obj_dev
    rows = cap + cap // fold
    extra = size_k * (size_k + 1) // 2 - LANES
    wide = LANES + -(-extra // 16) * 16
    assert n_band == 2 and 2 * obj_dev == LANES and 0 <= extra and extra + size_k < GROUP
    shape = jax.ShapeDtypeStruct
    chunk = max(c for c in range(LANES, 1024, LANES) if pix % c == 0)

    pixels = jnp.transpose(stamps, (1, 0, 2))
    payload = call(
        pack_kernel,
        shape((n_sky, 16, LANES), f32),
        [
            pltpu.VMEM((size_k, obj_dev), f32),
            pltpu.VMEM((nei, obj_dev), jnp.int32),
            pltpu.VMEM((nei, obj_dev), f32),
            pltpu.SemaphoreType.DMA((3,)),
        ],
        "hhh",
    )(hbm(theta_init), hbm(nb_id.T), hbm(nb_weight.T))
    got = lax.all_to_all(payload, "sky", 0, 0, tiled=True)
    tpl, pair, sel, spread, full, base, tag, gain, owner = call(
        functools.partial(ready_kernel, (n_sky, cap, obj_dev, extra)),
        (
            shape((bands, 2 * size_k, pix), bf16),
            shape((bands, wide, pix), bf16),
            shape((total, stamp_dev), bf16),
            shape((3 * size_k, 4 * LANES), bf16),
            shape((size_k * size_k + size_k, 2 * LANES), bf16),
            shape((stamp_dev, LANES), f32),
            shape((stamp_dev, LANES), f32),
            shape((8, stamp_dev), f32),
            shape((8, stamp_dev), jnp.int32),
        ),
        [
            pltpu.VMEM((1, stamp_dev), jnp.int32),
            pltpu.VMEM((1, stamp_dev), jnp.int32),
            pltpu.VMEM((1, stamp_dev), bf16),
            pltpu.VMEM((1, stamp_dev), bf16),
            pltpu.SemaphoreType.DMA((6,)),
        ],
        "hhhhhh",
    )(
        hbm(stamp_dest.T),
        hbm(stamp_obj[None, :]),
        hbm(stamp_gain[None, :]),
        hbm(stamp_invvar[None, :]),
        hbm(phi_tpl),
        hbm(psi_tpl),
    )
    everyone, hot, blend = call(
        functools.partial(index_kernel, nei),
        (
            shape((n_sky, 8, LANES), f32),
            shape((n_all, stamp_dev), bf16),
            shape((n_all, 2 * stamp_dev), bf16),
        ),
        [pltpu.VMEM((16, n_all), f32)],
    )(got, owner)
    terms = call(
        functools.partial(terms_kernel, (n_sky, cap, fold, chunk, extra)),
        shape((n_sky, rows, LANES), f32),
        [
            pltpu.VMEM((size_k, n_all), f32),
            pltpu.VMEM((stamp_dev, 2 * LANES), f32),
            pltpu.VMEM((stamp_dev, LANES), f32),
            pltpu.VMEM((stamp_dev, 2 * size_k), bf16),
            pltpu.VMEM((bands, stamp_dev, pix), bf16),
            pltpu.SemaphoreType.DMA((bands * (pix // chunk),)),
        ],
        "vvvvvvhvvvv",
    )
    theta = theta_init
    member = None
    for sweep in range(ITERS):
        sent = terms(
            everyone, hot, blend, gain, base, tag, hbm(pixels), tpl, pair, sel, spread
        )
        recv = lax.all_to_all(sent, "sky", 0, 0, tiled=True)
        other = lax.ppermute(recv, "band", [(0, 1), (1, 0)])
        learn, last = sweep == 0, sweep + 1 == ITERS
        sizes = (n_sky, cap, fold, n_band, extra + size_k, learn)

        def solve(*refs, learn=learn, last=last, sizes=sizes):
            refs = list(refs)
            if learn:
                refs.insert(2, None)
            if last:
                refs.insert(6, None)
            if not learn:
                refs.insert(8, None)
            solve_kernel(sizes, *refs)

        outs = [shape((n_sky, 8, LANES), f32)] * (not last)
        outs += [shape((size_k, obj_dev), f32)]
        outs += [shape((obj_dev, total), bf16)] * learn
        given = [recv, other] + [member] * (not learn) + [full, theta, theta_init]
        outs = call(solve, outs, [pltpu.VMEM((total, 2 * LANES), f32)])(*given)
        theta = outs[0 if last else 1]
        if learn:
            member = outs[-1]
        if not last:
            everyone = lax.all_to_all(outs[0], "sky", 0, 0, tiled=True)
    return theta


def solution(mesh):
    in_specs = (
        P("sky", "band", None),
        P("sky"),
        P("sky"),
        P("sky", None),
        P("sky"),
        P("band", None, None),
        P("band", None, None),
        P(None, "sky"),
        P("sky", None),
        P("sky", None),
    )
    out_specs = P(None, "sky")
    return jax.shard_map(local, mesh=mesh, in_specs=in_specs, out_specs=out_specs, check_vma=False)
```

time: 137 us -> 117 us (0.85)
  Pallas kernels: 46 us -> 34.9 us
  local copies, waits for them, and re-layouts: 8.98 us -> 2.46 us
  other arithmetic: 2.69 us -> 0 us
    pallas_call x9, Pallas kernels: 46 us -> 34.9 us  [the longest x3 25.1 us: local(): terms(everyone, hot, blend, gain, base, tag, hbm(pixels), tpl, pair, sel,...]
    unnamed x28 -> x2, local copies, waits for them, and re-layouts: 8.98 us -> 0.01 us
    broadcast_in_dim x0 -> x2, local copies, waits for them, and re-layouts: none -> 2.46 us  [the longest x1 1.23 us: local(): stamp_invvar[None, :]]
  transfers between devices with their start and end apart: 4 -> 4, of which waited for: 4 -> 4; matrix products, arithmetic and copies ran while one was open for 0% -> 2% of each run, Pallas kernels for 2% -> 3%
where the time goes in v1:
time: 117 us; the launch traced here: 116 us
  blocking collectives  63.7 us (54%)
  Pallas kernels  34.9 us (30%)
  starting transfers between devices  8.36 us (7%)
  waiting for transfers between devices  6.56 us (6%)
  local copies, waits for them, and re-layouts  2.46 us (2%)
    all_to_all x3, blocking collectives, local(): recv = lax.all_to_all(sent, 'sky', 0, 0, tiled=True)  42.1 us
    pallas_call x3, Pallas kernels, local(): terms(everyone, hot, blend, gain, base, tag, hbm(pixels), tpl, pair, sel,...  25.1 us
    all_to_all x2, blocking collectives, local(): everyone = lax.all_to_all(outs[0], 'sky', 0, 0, tiled=True)  21.6 us
    all_to_all x1, starting transfers between devices, local(): got = lax.all_to_all(payload, 'sky', 0, 0, tiled=True)  8.35 us
    ppermute x3, waiting for transfers between devices, local(): other = lax.ppermute(recv, 'band', [(0, 1), (1, 0)])  4.88 us
    pallas_call x3, Pallas kernels, local(): outs = call(solve, outs, [pltpu.VMEM((total, 2 * LANES), f32)])(*given)  3.71 us
    pallas_call x1, Pallas kernels, local(): call(functools.partial(ready_kernel, (n_sky, cap, obj_dev, extra)), (shap...  3.65 us
  transfers between devices with their start and end apart: 4, of which 4 were waited for; matrix products, arithmetic and copies ran while one was open for 2% of the time, Pallas kernels for 3%

profile of v1, /device:TPU:0, one launch (start us, length us, event | category | flops | bytes accessed | tf_op | source)
XLA Modules:
  0.0 116.1 jit_solution(17952742911695938745)
XLA Ops:
  0.0 1.5 %shard_map.100 = f32[16,16,128]{2,1,0:T(8,128)} custom-call(f32[16,64]{1,0:T(8,128)} %refs_5_.3, s32[4,64]{1,0:T(4,128)} %bitcast.8, f32[4,64]{1,0:T(4,128)} %bitcast.9), custom_call_target="tpu_custom_call" | custom-call | tf_op jit(solution)/shard_map/pallas_call | solution.py:448
  1.5 8.4 %all-to-all-start = ((f32[16,16,128]{2,1,0:T(8,128)}), f32[16,16,128]{2,1,0:T(8,128)S(1)}, u32[]{:S(2)}, u32[]{:S(2)}) async-start(f32[16,16,128]{2,1,0:T(8,128)} %shard_map.100), calls=%async_computation | async-start | bytes 262144 | tf_op jit(solution)/shard_map/all_to_all | solution.py:459
  9.8 1.2 %broadcast_in_dim.10.gain_hbm = bf16[1,256]{1,0:T(2,128)(2,1)} reshape(bf16[256]{0:T(256)(128)(2,1)} %param.11) | data formatting | bytes 1024 | tf_op jit(solution)/shard_map/broadcast_in_dim | solution.py:484
  11.1 1.2 %broadcast_in_dim.11.invvar_hbm = bf16[1,256]{1,0:T(2,128)(2,1)} reshape(bf16[256]{0:T(256)(128)(2,1)} %param.12) | data formatting | bytes 1024 | tf_op jit(solution)/shard_map/broadcast_in_dim | solution.py:485
  12.3 3.7 %shard_map.101 = (bf16[3,32,2304]{2,1,0:T(8,128)(2,1)S(1)}, bf16[3,144,2304]{2,1,0:T(8,128)(2,1)S(1)}, bf16[512,256]{1,0:T(8,128)(2,1)S(1)}, bf16[48,512]{1,0:T(...) custom-call(s32[1,256]{1,0:T(1,128)} %bitcast.10, ...), custom_call_target="tpu_custom_call" | custom-call | tf_op jit(solution)/shard_map/pallas_call | solution.py:460
  15.9 1.7 %all-to-all-done.got_ref = f32[16,16,128]{2,1,0:T(8,128)S(1)} async-done(((f32[16,16,128]{2,1,0:T(8,128)}), f32[16,16,128]{2,1,0:T(8,128)S(1)}, u32[]{:S(2)}, u32[]{:S(2)}) %all-to-all-start) | async-done | bytes 131104 | tf_op jit(solution)/shard_map/all_to_all | solution.py:459
  17.6 1.0 shard_map.102
  18.6 0.0 copy-start
  18.6 8.4 %shard_map.103 = f32[16,40,128]{2,1,0:T(8,128)S(1)} custom-call(f32[16,8,128]{2,1,0:T(8,128)S(1)} %get-tuple-element.23.theta_ref, bf16[1024,256]{1,0:T(8,128)(2,1)S(1)} %get-tuple-element.24.hot_ref, bf16[1024,512]{1,0:T(8,128)(2,1)S(1)} %get-tuple-element.25.blend_ref, f32[8,256]{1,0:T(8,128)S(1)} %get-tuple-element.26.gain_ref, ...), custom_call_target="tpu_custom_call" | custom-call | tf_op jit(solution)/shard_map/pallas_call | solution.py:514
  27.0 15.8 %all_to_all.30.refs_0_ = f32[16,40,128]{2,1,0:T(8,128)S(1)} all-to-all(f32[16,40,128]{2,1,0:T(8,128)S(1)} %shard_map.103), channel_id=1, replica_groups=mesh['sky'=16,'band'=2] {'sky'}, dimensions={0} | all-to-all | bytes 655360 | tf_op jit(solution)/shard_map/all_to_all | solution.py:517
  42.8 0.0 collective-permute-start
  42.8 1.6 %collective-permute-done.refs_1_ = f32[16,40,128]{2,1,0:T(8,128)S(1)} collective-permute-done((f32[16,40,128]{2,1,0:T(8,128)S(1)}, f32[16,40,128]{2,1,0:T(8,128)S(1)}, u32[]{:S(2)}, u32[]{:S(2)}) %collective-permute-start) | collective-permute-done | bytes 327712 | tf_op jit(solution)/shard_map/ppermute | solution.py:518
  44.4 1.2 %shard_map.104 = (f32[16,8,128]{2,1,0:T(8,128)S(1)}, f32[16,64]{1,0:T(8,128)S(1)}, bf16[64,512]{1,0:T(8,128)(2,1)S(1)}) custom-call(f32[16,40,128]{2,1,0:T(8,128)S(1)} %all_to_all.30.refs_0_, f32[16,40,128]{2,1,0:T(8,128)S(1)} %collective-permute-done.refs_1_, bf16[272,256]{1,0:T(8,128)(2,1)S(1)} %get-tuple-element.33.refs_2_.refs_3_, f32[16,64]{1,0:T(8,128)S(1)} %copy-done, ...), custom_call_target="tpu_custom_call" | custom-call | tf_op jit(solution)/shard_map/pallas_call | solution.py:536
  45.7 10.8 %all_to_all.31.theta_ref = f32[16,8,128]{2,1,0:T(8,128)S(1)} all-to-all(f32[16,8,128]{2,1,0:T(8,128)S(1)} %get-tuple-element.34), channel_id=1, replica_groups=mesh['sky'=16,'band'=2] {'sky'}, dimensions={0} | all-to-all | bytes 131072 | tf_op jit(solution)/shard_map/all_to_all | solution.py:541
  56.5 8.4 %shard_map.105 = f32[16,40,128]{2,1,0:T(8,128)S(1)} custom-call(f32[16,8,128]{2,1,0:T(8,128)S(1)} %all_to_all.31.theta_ref, bf16[1024,256]{1,0:T(8,128)(2,1)S(1)} %get-tuple-element.24.hot_ref, bf16[1024,512]{1,0:T(8,128)(2,1)S(1)} %get-tuple-element.25.blend_ref, f32[8,256]{1,0:T(8,128)S(1)} %get-tuple-element.26.gain_ref, ...), custom_call_target="tpu_custom_call" | custom-call | tf_op jit(solution)/shard_map/pallas_call | solution.py:514
  64.9 13.2 %all_to_all.32.refs_0_ = f32[16,40,128]{2,1,0:T(8,128)S(1)} all-to-all(f32[16,40,128]{2,1,0:T(8,128)S(1)} %shard_map.105), channel_id=1, replica_groups=mesh['sky'=16,'band'=2] {'sky'}, dimensions={0} | all-to-all | bytes 655360 | tf_op jit(solution)/shard_map/all_to_all | solution.py:517
  78.0 0.0 collective-permute-start.1
  78.0 1.6 %collective-permute-done.1.refs_1_ = f32[16,40,128]{2,1,0:T(8,128)S(1)} collective-permute-done((f32[16,40,128]{2,1,0:T(8,128)S(1)}, f32[16,40,128]{2,1,0:T(8,128)S(1)}, u32[]{:S(2)}, u32[]{:S(2)}) %collective-permute-start.1) | collective-permute-done | bytes 327712 | tf_op jit(solution)/shard_map/ppermute | solution.py:518
  79.7 0.9 shard_map.106
  80.6 10.8 %all_to_all.33.theta_ref = f32[16,8,128]{2,1,0:T(8,128)S(1)} all-to-all(f32[16,8,128]{2,1,0:T(8,128)S(1)} %get-tuple-element.37), channel_id=1, replica_groups=mesh['sky'=16,'band'=2] {'sky'}, dimensions={0} | all-to-all | bytes 131072 | tf_op jit(solution)/shard_map/all_to_all | solution.py:541
  91.4 8.4 %shard_map.107 = f32[16,40,128]{2,1,0:T(8,128)S(1)} custom-call(f32[16,8,128]{2,1,0:T(8,128)S(1)} %all_to_all.33.theta_ref, bf16[1024,256]{1,0:T(8,128)(2,1)S(1)} %get-tuple-element.24.hot_ref, bf16[1024,512]{1,0:T(8,128)(2,1)S(1)} %get-tuple-element.25.blend_ref, f32[8,256]{1,0:T(8,128)S(1)} %get-tuple-element.26.gain_ref, ...), custom_call_target="tpu_custom_call" | custom-call | tf_op jit(solution)/shard_map/pallas_call | solution.py:514
  99.8 13.2 %all_to_all.34.refs_0_ = f32[16,40,128]{2,1,0:T(8,128)S(1)} all-to-all(f32[16,40,128]{2,1,0:T(8,128)S(1)} %shard_map.107), channel_id=1, replica_groups=mesh['sky'=16,'band'=2] {'sky'}, dimensions={0} | all-to-all | bytes 655360 | tf_op jit(solution)/shard_map/all_to_all | solution.py:517
  113.0 1.6 %collective-permute-done.2.refs_1_ = f32[16,40,128]{2,1,0:T(8,128)S(1)} collective-permute-done((f32[16,40,128]{2,1,0:T(8,128)S(1)}, f32[16,40,128]{2,1,0:T(8,128)S(1)}, u32[]{:S(2)}, u32[]{:S(2)}) %collective-permute-start.2) | collective-permute-done | bytes 327712 | tf_op jit(solution)/shard_map/ppermute | solution.py:518
  114.6 1.5 %shard_map.108 = f32[16,64]{1,0:T(8,128)} custom-call(f32[16,40,128]{2,1,0:T(8,128)S(1)} %all_to_all.34.refs_0_, f32[16,40,128]{2,1,0:T(8,128)S(1)} %collective-permute-done.2.refs_1_, bf16[64,512]{1,0:T(8,128)(2,1)S(1)} %get-tuple-element.35.refs_2_, bf16[272,256]{1,0:T(8,128)(2,1)S(1)} %get-tuple-element.33.refs_2_.refs_3_, ...), custom_call_target="tpu_custom_call" | custom-call | tf_op jit(solution)/shard_map/pallas_call | solution.py:536
  (2 shorter events, 0.0 us)
Async XLA Ops:
  1.5 16.2 %all-to-all-start = ((f32[16,16,128]{2,1,0:T(8,128)}), f32[16,16,128]{2,1,0:T(8,128)S(1)}, u32[]{:S(2)}, u32[]{:S(2)}) async-start(f32[16,16,128]{2,1,0:T(8,128)} %shard_map.100), calls=%async_computation | async-start | bytes 262144 | tf_op jit(solution)/shard_map/all_to_all | solution.py:459
  18.6 25.8 %copy-start = (f32[16,64]{1,0:T(8,128)S(1)}, f32[16,64]{1,0:T(8,128)}, u32[]{:S(2)}) copy-start(f32[16,64]{1,0:T(8,128)} %refs_5_.3) | copy-start | bytes 12292
  42.8 1.6 %collective-permute-start = (f32[16,40,128]{2,1,0:T(8,128)S(1)}, f32[16,40,128]{2,1,0:T(8,128)S(1)}, u32[]{:S(2)}, u32[]{:S(2)}) collective-permute-start(f32[16,40,128]{2,1,0:T(8,128)S(1)} %all_to_all.30.refs_0_), channel_id=1, source_target_pairs={{0,1},{1,0},{2,3},{3,2},{4,5},{5,4},{6,7},{7,6},{8,9},{9,8},{10,11... | collective-permute-start | bytes 983048 | tf_op jit(solution)/shard_map/ppermute | solution.py:518
  78.0 1.6 %collective-permute-start.1 = (f32[16,40,128]{2,1,0:T(8,128)S(1)}, f32[16,40,128]{2,1,0:T(8,128)S(1)}, u32[]{:S(2)}, u32[]{:S(2)}) collective-permute-start(f32[16,40,128]{2,1,0:T(8,128)S(1)} %all_to_all.32.refs_0_), channel_id=1, source_target_pairs={{0,1},{1,0},{2,3},{3,2},{4,5},{5,4},{6,7},{7,6},{8,9},{9,8},{10,11... | collective-permute-start | bytes 983048 | tf_op jit(solution)/shard_map/ppermute | solution.py:518
  113.0 1.6 %collective-permute-start.2 = (f32[16,40,128]{2,1,0:T(8,128)S(1)}, f32[16,40,128]{2,1,0:T(8,128)S(1)}, u32[]{:S(2)}, u32[]{:S(2)}) collective-permute-start(f32[16,40,128]{2,1,0:T(8,128)S(1)} %all_to_all.34.refs_0_), channel_id=1, source_target_pairs={{0,1},{1,0},{2,3},{3,2},{4,5},{5,4},{6,7},{7,6},{8,9},{9,8},{10,11... | collective-permute-start | bytes 983048 | tf_op jit(solution)/shard_map/ppermute | solution.py:518

commit v2 on v1

--- a/solution.py
+++ b/solution.py
@@ -182,7 +182,10 @@
     return jnp.where(lane < LANES // 2, pltpu.roll(x, LANES // 2, 1), y)
 
 
-def index_kernel(nei, got_ref, owner_ref, theta_ref, hot_ref, blend_ref, table_ref):
+def index_kernel(
+    nei, got_ref, owner_ref, pix_hbm, theta_ref, hot_ref, blend_ref, pix_ref, table_ref, sem
+):
+    load = dma([pltpu.make_async_copy(pix_hbm, pix_ref, sem)])
     n_sky = got_ref.shape[0]
     n_all, stamps = hot_ref.shape
     block = LANES
@@ -220,6 +223,7 @@
         return carry
 
     lax.fori_loop(0, n_all // block, blend, 0)
+    wait(load)
 
 
 def terms_kernel(
@@ -230,7 +234,7 @@
     gain_ref,
     base_ref,
     tag_ref,
-    pix_hbm,
+    pix_ref,
     tpl_ref,
     pair_ref,
     sel_ref,
@@ -240,8 +244,6 @@
     acc_ref,
     proj_ref,
     lit_ref,
-    pix_ref,
-    sem,
 ):
     n_sky, cap, fold, chunk, extra = sizes
     bands, stamps, pix = pix_ref.shape
@@ -249,12 +251,6 @@
     steps = [
         (b, slice(c * chunk, (c + 1) * chunk)) for b in range(bands) for c in range(pix // chunk)
     ]
-    loads = dma(
-        [
-            pltpu.make_async_copy(pix_hbm.at[b, :, px], pix_ref.at[b, :, px], sem.at[i])
-            for i, (b, px) in enumerate(steps)
-        ]
-    )
     lane = iota((8, LANES), 1)
     for i in range(n_sky // 2):
         span = slice(i * LANES, (i + 1) * LANES)
@@ -293,7 +289,6 @@
     held = None
     for i, here in enumerate(steps):
         ahead = model(*steps[i + 1]) if i + 1 < len(steps) else None
-        loads[i].wait()
         now = weigh(*here, light)
         if held is not None:
             gather(*steps[i - 1], *held)
@@ -486,15 +481,17 @@
         hbm(phi_tpl),
         hbm(psi_tpl),
     )
-    everyone, hot, blend = call(
+    everyone, hot, blend, pixels = call(
         functools.partial(index_kernel, nei),
         (
             shape((n_sky, 8, LANES), f32),
             shape((n_all, stamp_dev), bf16),
             shape((n_all, 2 * stamp_dev), bf16),
+            shape((bands, stamp_dev, pix), bf16),
         ),
-        [pltpu.VMEM((16, n_all), f32)],
-    )(got, owner)
+        [pltpu.VMEM((16, n_all), f32), pltpu.SemaphoreType.DMA(())],
+        "vvh",
+    )(got, owner, hbm(pixels))
     terms = call(
         functools.partial(terms_kernel, (n_sky, cap, fold, chunk, extra)),
         shape((n_sky, rows, LANES), f32),
@@ -503,16 +500,13 @@
             pltpu.VMEM((stamp_dev, 2 * LANES), f32),
             pltpu.VMEM((stamp_dev, LANES), f32),
             pltpu.VMEM((stamp_dev, 2 * size_k), bf16),
-            pltpu.VMEM((bands, stamp_dev, pix), bf16),
-            pltpu.SemaphoreType.DMA((bands * (pix // chunk),)),
         ],
-        "vvvvvvhvvvv",
     )
     theta = theta_init
     member = None
     for sweep in range(ITERS):
         sent = terms(
-            everyone, hot, blend, gain, base, tag, hbm(pixels), tpl, pair, sel, spread
+            everyone, hot, blend, gain, base, tag, pixels, tpl, pair, sel, spread
         )
         recv = lax.all_to_all(sent, "sky", 0, 0, tiled=True)
         other = lax.ppermute(recv, "band", [(0, 1), (1, 0)])

time: 117 us -> 107 us (0.915)
  Pallas kernels: 34.9 us -> 25.5 us
    pallas_call x3, Pallas kernels: 25.1 us -> 14.6 us  [local(): terms(everyone, hot, blend, gain, base, tag, pixels, tpl, pair, sel, spread)]
where the time goes in v2:
time: 107 us
  blocking collectives  63.7 us (60%)
  Pallas kernels  25.5 us (24%)
  starting transfers between devices  8.36 us (8%)
  waiting for transfers between devices  6.56 us (6%)
  local copies, waits for them, and re-layouts  2.46 us (2%)
    all_to_all x3, blocking collectives, local(): recv = lax.all_to_all(sent, 'sky', 0, 0, tiled=True)  42.1 us
    all_to_all x2, blocking collectives, local(): everyone = lax.all_to_all(outs[0], 'sky', 0, 0, tiled=True)  21.6 us
    pallas_call x3, Pallas kernels, local(): terms(everyone, hot, blend, gain, base, tag, pixels, tpl, pair, sel, spread)  14.6 us
    all_to_all x1, starting transfers between devices, local(): got = lax.all_to_all(payload, 'sky', 0, 0, tiled=True)  8.35 us
    ppermute x3, waiting for transfers between devices, local(): other = lax.ppermute(recv, 'band', [(0, 1), (1, 0)])  4.88 us
    pallas_call x3, Pallas kernels, local(): outs = call(solve, outs, [pltpu.VMEM((total, 2 * LANES), f32)])(*given)  3.71 us
    pallas_call x1, Pallas kernels, local(): call(functools.partial(ready_kernel, (n_sky, cap, obj_dev, extra)), (shap...  3.65 us
  transfers between devices with their start and end apart: 4, of which 4 were waited for; matrix products, arithmetic and copies ran while one was open for 2% of the time, Pallas kernels for 3%

profile of v2, /device:TPU:0, one launch (start us, length us, event | category | flops | bytes accessed | tf_op | source)
XLA Modules:
  0.0 106.6 jit_solution(15395604068778049093)
XLA Ops:
  0.0 1.5 %shard_map.100 = f32[16,16,128]{2,1,0:T(8,128)} custom-call(f32[16,64]{1,0:T(8,128)} %refs_5_.3, s32[4,64]{1,0:T(4,128)} %bitcast.6, f32[4,64]{1,0:T(4,128)} %bitcast.7), custom_call_target="tpu_custom_call" | custom-call | tf_op jit(solution)/shard_map/pallas_call | solution.py:443
  1.5 8.4 %all-to-all-start = ((f32[16,16,128]{2,1,0:T(8,128)}), f32[16,16,128]{2,1,0:T(8,128)S(1)}, u32[]{:S(2)}, u32[]{:S(2)}) async-start(f32[16,16,128]{2,1,0:T(8,128)} %shard_map.100), calls=%async_computation | async-start | bytes 262144 | tf_op jit(solution)/shard_map/all_to_all | solution.py:454
  9.8 1.2 %broadcast_in_dim.10.gain_hbm = bf16[1,256]{1,0:T(2,128)(2,1)} reshape(bf16[256]{0:T(256)(128)(2,1)} %param.11) | data formatting | bytes 1024 | tf_op jit(solution)/shard_map/broadcast_in_dim | solution.py:479
  11.1 1.2 %broadcast_in_dim.11.invvar_hbm = bf16[1,256]{1,0:T(2,128)(2,1)} reshape(bf16[256]{0:T(256)(128)(2,1)} %param.12) | data formatting | bytes 1024 | tf_op jit(solution)/shard_map/broadcast_in_dim | solution.py:480
  12.3 3.7 %shard_map.101 = (bf16[3,32,2304]{2,1,0:T(8,128)(2,1)S(1)}, bf16[3,144,2304]{2,1,0:T(8,128)(2,1)S(1)}, bf16[512,256]{1,0:T(8,128)(2,1)S(1)}, bf16[48,512]{1,0:T(...) custom-call(s32[1,256]{1,0:T(1,128)} %bitcast.8, ...), custom_call_target="tpu_custom_call" | custom-call | tf_op jit(solution)/shard_map/pallas_call | solution.py:455
  15.9 1.7 %all-to-all-done.got_ref = f32[16,16,128]{2,1,0:T(8,128)S(1)} async-done(((f32[16,16,128]{2,1,0:T(8,128)}), f32[16,16,128]{2,1,0:T(8,128)S(1)}, u32[]{:S(2)}, u32[]{:S(2)}) %all-to-all-start) | async-done | bytes 131104 | tf_op jit(solution)/shard_map/all_to_all | solution.py:454
  17.6 2.0 %shard_map.102 = (f32[16,8,128]{2,1,0:T(8,128)S(1)}, bf16[1024,256]{1,0:T(8,128)(2,1)S(1)}, bf16[1024,512]{1,0:T(8,128)(2,1)S(1)}, bf16[3,256,2304]{2,1,0:T(8,128)(2,1)S(1)}) custom-call(f32[16,16,128]{2,1,0:T(8,128)S(1)} %all-to-all-done.got_ref, s32[8,256]{1,0:T(8,128)S(1)} %get-tuple-element.23.owner_ref, bf16[3,256,2304]{2,1,0:T(8,128)(2,1)} %bitcast.5), custom_call_target="tpu_custom_call" | custom-call | tf_op jit(solution)/shard_map/pallas_call | solution.py:484
  19.6 0.0 copy-start
  19.7 4.9 %shard_map.103 = f32[16,40,128]{2,1,0:T(8,128)S(1)} custom-call(f32[16,8,128]{2,1,0:T(8,128)S(1)} %get-tuple-element.24.theta_ref, bf16[1024,256]{1,0:T(8,128)(2,1)S(1)} %get-tuple-element.25.hot_ref, bf16[1024,512]{1,0:T(8,128)(2,1)S(1)} %get-tuple-element.26.blend_ref, f32[8,256]{1,0:T(8,128)S(1)} %get-tuple-element.27.gain_ref, ...), custom_call_target="tpu_custom_call" | custom-call | tf_op jit(solution)/shard_map/pallas_call | solution.py:508
  24.5 15.8 %all_to_all.30.refs_0_ = f32[16,40,128]{2,1,0:T(8,128)S(1)} all-to-all(f32[16,40,128]{2,1,0:T(8,128)S(1)} %shard_map.103), channel_id=1, replica_groups=mesh['sky'=16,'band'=2] {'sky'}, dimensions={0} | all-to-all | bytes 655360 | tf_op jit(solution)/shard_map/all_to_all | solution.py:511
  40.3 0.0 collective-permute-start
  40.3 1.6 %collective-permute-done.refs_1_ = f32[16,40,128]{2,1,0:T(8,128)S(1)} collective-permute-done((f32[16,40,128]{2,1,0:T(8,128)S(1)}, f32[16,40,128]{2,1,0:T(8,128)S(1)}, u32[]{:S(2)}, u32[]{:S(2)}) %collective-permute-start) | collective-permute-done | bytes 327712 | tf_op jit(solution)/shard_map/ppermute | solution.py:512
  42.0 1.2 %shard_map.104 = (f32[16,8,128]{2,1,0:T(8,128)S(1)}, f32[16,64]{1,0:T(8,128)S(1)}, bf16[64,512]{1,0:T(8,128)(2,1)S(1)}) custom-call(f32[16,40,128]{2,1,0:T(8,128)S(1)} %all_to_all.30.refs_0_, f32[16,40,128]{2,1,0:T(8,128)S(1)} %collective-permute-done.refs_1_, bf16[272,256]{1,0:T(8,128)(2,1)S(1)} %get-tuple-element.35.refs_2_.refs_3_, f32[16,64]{1,0:T(8,128)S(1)} %copy-done, ...), custom_call_target="tpu_custom_call" | custom-call | tf_op jit(solution)/shard_map/pallas_call | solution.py:530
  43.2 10.8 %all_to_all.31.theta_ref = f32[16,8,128]{2,1,0:T(8,128)S(1)} all-to-all(f32[16,8,128]{2,1,0:T(8,128)S(1)} %get-tuple-element.36), channel_id=1, replica_groups=mesh['sky'=16,'band'=2] {'sky'}, dimensions={0} | all-to-all | bytes 131072 | tf_op jit(solution)/shard_map/all_to_all | solution.py:535
  54.0 4.9 %shard_map.105 = f32[16,40,128]{2,1,0:T(8,128)S(1)} custom-call(f32[16,8,128]{2,1,0:T(8,128)S(1)} %all_to_all.31.theta_ref, bf16[1024,256]{1,0:T(8,128)(2,1)S(1)} %get-tuple-element.25.hot_ref, bf16[1024,512]{1,0:T(8,128)(2,1)S(1)} %get-tuple-element.26.blend_ref, f32[8,256]{1,0:T(8,128)S(1)} %get-tuple-element.27.gain_ref, ...), custom_call_target="tpu_custom_call" | custom-call | tf_op jit(solution)/shard_map/pallas_call | solution.py:508
  58.9 13.1 %all_to_all.32.refs_0_ = f32[16,40,128]{2,1,0:T(8,128)S(1)} all-to-all(f32[16,40,128]{2,1,0:T(8,128)S(1)} %shard_map.105), channel_id=1, replica_groups=mesh['sky'=16,'band'=2] {'sky'}, dimensions={0} | all-to-all | bytes 655360 | tf_op jit(solution)/shard_map/all_to_all | solution.py:511
  72.1 0.0 collective-permute-start.1
  72.1 1.6 %collective-permute-done.1.refs_1_ = f32[16,40,128]{2,1,0:T(8,128)S(1)} collective-permute-done((f32[16,40,128]{2,1,0:T(8,128)S(1)}, f32[16,40,128]{2,1,0:T(8,128)S(1)}, u32[]{:S(2)}, u32[]{:S(2)}) %collective-permute-start.1) | collective-permute-done | bytes 327712 | tf_op jit(solution)/shard_map/ppermute | solution.py:512
  73.7 0.9 shard_map.106
  74.6 10.8 %all_to_all.33.theta_ref = f32[16,8,128]{2,1,0:T(8,128)S(1)} all-to-all(f32[16,8,128]{2,1,0:T(8,128)S(1)} %get-tuple-element.39), channel_id=1, replica_groups=mesh['sky'=16,'band'=2] {'sky'}, dimensions={0} | all-to-all | bytes 131072 | tf_op jit(solution)/shard_map/all_to_all | solution.py:535
  85.4 4.9 %shard_map.107 = f32[16,40,128]{2,1,0:T(8,128)S(1)} custom-call(f32[16,8,128]{2,1,0:T(8,128)S(1)} %all_to_all.33.theta_ref, bf16[1024,256]{1,0:T(8,128)(2,1)S(1)} %get-tuple-element.25.hot_ref, bf16[1024,512]{1,0:T(8,128)(2,1)S(1)} %get-tuple-element.26.blend_ref, f32[8,256]{1,0:T(8,128)S(1)} %get-tuple-element.27.gain_ref, ...), custom_call_target="tpu_custom_call" | custom-call | tf_op jit(solution)/shard_map/pallas_call | solution.py:508
  90.3 13.2 %all_to_all.34.refs_0_ = f32[16,40,128]{2,1,0:T(8,128)S(1)} all-to-all(f32[16,40,128]{2,1,0:T(8,128)S(1)} %shard_map.107), channel_id=1, replica_groups=mesh['sky'=16,'band'=2] {'sky'}, dimensions={0} | all-to-all | bytes 655360 | tf_op jit(solution)/shard_map/all_to_all | solution.py:511
  103.5 1.6 %collective-permute-done.2.refs_1_ = f32[16,40,128]{2,1,0:T(8,128)S(1)} collective-permute-done((f32[16,40,128]{2,1,0:T(8,128)S(1)}, f32[16,40,128]{2,1,0:T(8,128)S(1)}, u32[]{:S(2)}, u32[]{:S(2)}) %collective-permute-start.2) | collective-permute-done | bytes 327712 | tf_op jit(solution)/shard_map/ppermute | solution.py:512
  105.1 1.5 %shard_map.108 = f32[16,64]{1,0:T(8,128)} custom-call(f32[16,40,128]{2,1,0:T(8,128)S(1)} %all_to_all.34.refs_0_, f32[16,40,128]{2,1,0:T(8,128)S(1)} %collective-permute-done.2.refs_1_, bf16[64,512]{1,0:T(8,128)(2,1)S(1)} %get-tuple-element.37.refs_2_, bf16[272,256]{1,0:T(8,128)(2,1)S(1)} %get-tuple-element.35.refs_2_.refs_3_, ...), custom_call_target="tpu_custom_call" | custom-call | tf_op jit(solution)/shard_map/pallas_call | solution.py:530
  (2 shorter events, 0.0 us)
Async XLA Ops:
  1.5 16.2 %all-to-all-start = ((f32[16,16,128]{2,1,0:T(8,128)}), f32[16,16,128]{2,1,0:T(8,128)S(1)}, u32[]{:S(2)}, u32[]{:S(2)}) async-start(f32[16,16,128]{2,1,0:T(8,128)} %shard_map.100), calls=%async_computation | async-start | bytes 262144 | tf_op jit(solution)/shard_map/all_to_all | solution.py:454
  19.6 22.3 %copy-start = (f32[16,64]{1,0:T(8,128)S(1)}, f32[16,64]{1,0:T(8,128)}, u32[]{:S(2)}) copy-start(f32[16,64]{1,0:T(8,128)} %refs_5_.3) | copy-start | bytes 12292
  40.3 1.6 %collective-permute-start = (f32[16,40,128]{2,1,0:T(8,128)S(1)}, f32[16,40,128]{2,1,0:T(8,128)S(1)}, u32[]{:S(2)}, u32[]{:S(2)}) collective-permute-start(f32[16,40,128]{2,1,0:T(8,128)S(1)} %all_to_all.30.refs_0_), channel_id=1, source_target_pairs={{0,1},{1,0},{2,3},{3,2},{4,5},{5,4},{6,7},{7,6},{8,9},{9,8},{10,11... | collective-permute-start | bytes 983048 | tf_op jit(solution)/shard_map/ppermute | solution.py:512
  72.1 1.6 %collective-permute-start.1 = (f32[16,40,128]{2,1,0:T(8,128)S(1)}, f32[16,40,128]{2,1,0:T(8,128)S(1)}, u32[]{:S(2)}, u32[]{:S(2)}) collective-permute-start(f32[16,40,128]{2,1,0:T(8,128)S(1)} %all_to_all.32.refs_0_), channel_id=1, source_target_pairs={{0,1},{1,0},{2,3},{3,2},{4,5},{5,4},{6,7},{7,6},{8,9},{9,8},{10,11... | collective-permute-start | bytes 983048 | tf_op jit(solution)/shard_map/ppermute | solution.py:512
  103.5 1.6 %collective-permute-start.2 = (f32[16,40,128]{2,1,0:T(8,128)S(1)}, f32[16,40,128]{2,1,0:T(8,128)S(1)}, u32[]{:S(2)}, u32[]{:S(2)}) collective-permute-start(f32[16,40,128]{2,1,0:T(8,128)S(1)} %all_to_all.34.refs_0_), channel_id=1, source_target_pairs={{0,1},{1,0},{2,3},{3,2},{4,5},{5,4},{6,7},{7,6},{8,9},{9,8},{10,11... | collective-permute-start | bytes 983048 | tf_op jit(solution)/shard_map/ppermute | solution.py:512

commit v3 on v2

--- a/solution.py
+++ b/solution.py
@@ -151,8 +151,10 @@
     wait(first)
     dest = dest_ref[...]
     obj = obj_ref[...]
-    gain_ref[...] = jnp.broadcast_to(gain_low_ref[...].astype(f32), gain_ref.shape)
-    base_ref[...] = jnp.broadcast_to(1.0 / invvar_ref[...].astype(f32), (LANES, stamps)).T
+    gain = gain_low_ref[...].astype(f32).reshape(1, stamps)
+    gain_ref[...] = jnp.broadcast_to(gain, gain_ref.shape)
+    variance = 1.0 / invvar_ref[...].astype(f32).reshape(1, stamps)
+    base_ref[...] = jnp.broadcast_to(variance, (LANES, stamps)).T
     named = jnp.broadcast_to((obj + 1).astype(f32), (LANES, stamps)).T
     tag_ref[...] = jnp.where(
         iota((stamps, LANES), 1) == extra + size_k, named, 0.0
@@ -185,9 +187,17 @@
 def index_kernel(
     nei, got_ref, owner_ref, pix_hbm, theta_ref, hot_ref, blend_ref, pix_ref, table_ref, sem
 ):
-    load = dma([pltpu.make_async_copy(pix_hbm, pix_ref, sem)])
+    bands, stamps = pix_ref.shape[:2]
+    half = stamps // 2
+    parts = [(b, slice(h * half, (h + 1) * half)) for b in range(bands) for h in range(2)]
+    load = dma(
+        [
+            pltpu.make_async_copy(pix_hbm.at[b, rows], pix_ref.at[b, rows], sem.at[i])
+            for i, (b, rows) in enumerate(parts)
+        ]
+    )
     n_sky = got_ref.shape[0]
-    n_all, stamps = hot_ref.shape
+    n_all = hot_ref.shape[0]
     block = LANES
     owner = owner_ref[0:1, :]
 
@@ -468,16 +478,16 @@
         [
             pltpu.VMEM((1, stamp_dev), jnp.int32),
             pltpu.VMEM((1, stamp_dev), jnp.int32),
-            pltpu.VMEM((1, stamp_dev), bf16),
-            pltpu.VMEM((1, stamp_dev), bf16),
+            pltpu.VMEM((stamp_dev,), bf16),
+            pltpu.VMEM((stamp_dev,), bf16),
             pltpu.SemaphoreType.DMA((6,)),
         ],
         "hhhhhh",
     )(
         hbm(stamp_dest.T),
         hbm(stamp_obj[None, :]),
-        hbm(stamp_gain[None, :]),
-        hbm(stamp_invvar[None, :]),
+        hbm(stamp_gain),
+        hbm(stamp_invvar),
         hbm(phi_tpl),
         hbm(psi_tpl),
     )
@@ -489,7 +499,7 @@
             shape((n_all, 2 * stamp_dev), bf16),
             shape((bands, stamp_dev, pix), bf16),
         ),
-        [pltpu.VMEM((16, n_all), f32), pltpu.SemaphoreType.DMA(())],
+        [pltpu.VMEM((16, n_all), f32), pltpu.SemaphoreType.DMA((2 * bands,))],
         "vvh",
     )(got, owner, hbm(pixels))
     terms = call(

time: 107 us -> 105 us (0.981)
  waiting for transfers between devices: 6.56 us -> 9.03 us
  local copies, waits for them, and re-layouts: 2.46 us -> 0.01 us
  blocking collectives: 63.7 us -> 61.3 us
    all_to_all x1, waiting for transfers between devices: 1.68 us -> 4.15 us  [local(): got = lax.all_to_all(payload, 'sky', 0, 0, tiled=True)]
    all_to_all x3, blocking collectives: 42.1 us -> 39.6 us  [local(): recv = lax.all_to_all(sent, 'sky', 0, 0, tiled=True)]
    broadcast_in_dim x2 -> x0, local copies, waits for them, and re-layouts: 2.46 us -> none  [the longest x1 1.23 us: local(): stamp_invvar[None, :]]
  transfers between devices with their start and end apart: 4 -> 4, of which waited for: 4 -> 4; matrix products, arithmetic and copies ran while one was open for 2% -> 0% of each run, Pallas kernels for 3% -> 3%
where the time goes in v3:
time: 105 us; the launch traced here: 104 us
  blocking collectives  61.3 us (58%)
  Pallas kernels  25.5 us (24%)
  waiting for transfers between devices  9.03 us (9%)
  starting transfers between devices  8.36 us (8%)
    all_to_all x3, blocking collectives, local(): recv = lax.all_to_all(sent, 'sky', 0, 0, tiled=True)  39.6 us
    all_to_all x2, blocking collectives, local(): everyone = lax.all_to_all(outs[0], 'sky', 0, 0, tiled=True)  21.6 us
    pallas_call x3, Pallas kernels, local(): terms(everyone, hot, blend, gain, base, tag, pixels, tpl, pair, sel, spread)  14.6 us
    all_to_all x1, starting transfers between devices, local(): got = lax.all_to_all(payload, 'sky', 0, 0, tiled=True)  8.35 us
    ppermute x3, waiting for transfers between devices, local(): other = lax.ppermute(recv, 'band', [(0, 1), (1, 0)])  4.88 us
    all_to_all x1, waiting for transfers between devices, local(): got = lax.all_to_all(payload, 'sky', 0, 0, tiled=True)  4.15 us
    pallas_call x3, Pallas kernels, local(): outs = call(solve, outs, [pltpu.VMEM((total, 2 * LANES), f32)])(*given)  3.71 us
    pallas_call x1, Pallas kernels, local(): call(functools.partial(ready_kernel, (n_sky, cap, obj_dev, extra)), (shap...  3.64 us
  transfers between devices with their start and end apart: 4, of which 4 were waited for; matrix products, arithmetic and copies ran while one was open for 0% of the time, Pallas kernels for 3%

profile of v3, /device:TPU:0, one launch (start us, length us, event | category | flops | bytes accessed | tf_op | source)
XLA Modules:
  0.0 104.2 jit_solution(16420988605172663709)
XLA Ops:
  0.0 1.5 %shard_map.100 = f32[16,16,128]{2,1,0:T(8,128)} custom-call(f32[16,64]{1,0:T(8,128)} %refs_5_.3, s32[4,64]{1,0:T(4,128)} %bitcast.6, f32[4,64]{1,0:T(4,128)} %bitcast.7), custom_call_target="tpu_custom_call" | custom-call | tf_op jit(solution)/shard_map/pallas_call | solution.py:453
  1.5 8.4 %all-to-all-start = ((f32[16,16,128]{2,1,0:T(8,128)}), f32[16,16,128]{2,1,0:T(8,128)S(1)}, u32[]{:S(2)}, u32[]{:S(2)}) async-start(f32[16,16,128]{2,1,0:T(8,128)} %shard_map.100), calls=%async_computation | async-start | bytes 262144 | tf_op jit(solution)/shard_map/all_to_all | solution.py:464
  9.8 3.6 %shard_map.101 = (bf16[3,32,2304]{2,1,0:T(8,128)(2,1)S(1)}, bf16[3,144,2304]{2,1,0:T(8,128)(2,1)S(1)}, bf16[512,256]{1,0:T(8,128)(2,1)S(1)}, bf16[48,512]{1,0:T(...) custom-call(s32[1,256]{1,0:T(1,128)} %bitcast.8, ...), custom_call_target="tpu_custom_call" | custom-call | tf_op jit(solution)/shard_map/pallas_call | solution.py:465
  13.5 4.1 %all-to-all-done.got_ref = f32[16,16,128]{2,1,0:T(8,128)S(1)} async-done(((f32[16,16,128]{2,1,0:T(8,128)}), f32[16,16,128]{2,1,0:T(8,128)S(1)}, u32[]{:S(2)}, u32[]{:S(2)}) %all-to-all-start) | async-done | bytes 131104 | tf_op jit(solution)/shard_map/all_to_all | solution.py:464
  17.6 2.0 %shard_map.102 = (f32[16,8,128]{2,1,0:T(8,128)S(1)}, bf16[1024,256]{1,0:T(8,128)(2,1)S(1)}, bf16[1024,512]{1,0:T(8,128)(2,1)S(1)}, bf16[3,256,2304]{2,1,0:T(8,128)(2,1)S(1)}) custom-call(f32[16,16,128]{2,1,0:T(8,128)S(1)} %all-to-all-done.got_ref, s32[8,256]{1,0:T(8,128)S(1)} %get-tuple-element.23.owner_ref, bf16[3,256,2304]{2,1,0:T(8,128)(2,1)} %bitcast.5), custom_call_target="tpu_custom_call" | custom-call | tf_op jit(solution)/shard_map/pallas_call | solution.py:494
  19.6 0.0 copy-start
  19.7 4.9 %shard_map.103 = f32[16,40,128]{2,1,0:T(8,128)S(1)} custom-call(f32[16,8,128]{2,1,0:T(8,128)S(1)} %get-tuple-element.24.theta_ref, bf16[1024,256]{1,0:T(8,128)(2,1)S(1)} %get-tuple-element.25.hot_ref, bf16[1024,512]{1,0:T(8,128)(2,1)S(1)} %get-tuple-element.26.blend_ref, f32[8,256]{1,0:T(8,128)S(1)} %get-tuple-element.27.gain_ref, ...), custom_call_target="tpu_custom_call" | custom-call | tf_op jit(solution)/shard_map/pallas_call | solution.py:518
  24.5 13.3 %all_to_all.30.refs_0_ = f32[16,40,128]{2,1,0:T(8,128)S(1)} all-to-all(f32[16,40,128]{2,1,0:T(8,128)S(1)} %shard_map.103), channel_id=1, replica_groups=mesh['sky'=16,'band'=2] {'sky'}, dimensions={0} | all-to-all | bytes 655360 | tf_op jit(solution)/shard_map/all_to_all | solution.py:521
  37.9 0.0 collective-permute-start
  37.9 1.6 %collective-permute-done.refs_1_ = f32[16,40,128]{2,1,0:T(8,128)S(1)} collective-permute-done((f32[16,40,128]{2,1,0:T(8,128)S(1)}, f32[16,40,128]{2,1,0:T(8,128)S(1)}, u32[]{:S(2)}, u32[]{:S(2)}) %collective-permute-start) | collective-permute-done | bytes 327712 | tf_op jit(solution)/shard_map/ppermute | solution.py:522
  39.5 0.0 copy-done
  39.5 1.2 %shard_map.104 = (f32[16,8,128]{2,1,0:T(8,128)S(1)}, f32[16,64]{1,0:T(8,128)S(1)}, bf16[64,512]{1,0:T(8,128)(2,1)S(1)}) custom-call(f32[16,40,128]{2,1,0:T(8,128)S(1)} %all_to_all.30.refs_0_, f32[16,40,128]{2,1,0:T(8,128)S(1)} %collective-permute-done.refs_1_, bf16[272,256]{1,0:T(8,128)(2,1)S(1)} %get-tuple-element.35.refs_2_.refs_3_, f32[16,64]{1,0:T(8,128)S(1)} %copy-done, ...), custom_call_target="tpu_custom_call" | custom-call | tf_op jit(solution)/shard_map/pallas_call | solution.py:540
  40.8 10.8 %all_to_all.31.theta_ref = f32[16,8,128]{2,1,0:T(8,128)S(1)} all-to-all(f32[16,8,128]{2,1,0:T(8,128)S(1)} %get-tuple-element.36), channel_id=1, replica_groups=mesh['sky'=16,'band'=2] {'sky'}, dimensions={0} | all-to-all | bytes 131072 | tf_op jit(solution)/shard_map/all_to_all | solution.py:545
  51.6 4.9 %shard_map.105 = f32[16,40,128]{2,1,0:T(8,128)S(1)} custom-call(f32[16,8,128]{2,1,0:T(8,128)S(1)} %all_to_all.31.theta_ref, bf16[1024,256]{1,0:T(8,128)(2,1)S(1)} %get-tuple-element.25.hot_ref, bf16[1024,512]{1,0:T(8,128)(2,1)S(1)} %get-tuple-element.26.blend_ref, f32[8,256]{1,0:T(8,128)S(1)} %get-tuple-element.27.gain_ref, ...), custom_call_target="tpu_custom_call" | custom-call | tf_op jit(solution)/shard_map/pallas_call | solution.py:518
  56.5 13.1 %all_to_all.32.refs_0_ = f32[16,40,128]{2,1,0:T(8,128)S(1)} all-to-all(f32[16,40,128]{2,1,0:T(8,128)S(1)} %shard_map.105), channel_id=1, replica_groups=mesh['sky'=16,'band'=2] {'sky'}, dimensions={0} | all-to-all | bytes 655360 | tf_op jit(solution)/shard_map/all_to_all | solution.py:521
  69.6 0.0 collective-permute-start.1
  69.6 1.6 %collective-permute-done.1.refs_1_ = f32[16,40,128]{2,1,0:T(8,128)S(1)} collective-permute-done((f32[16,40,128]{2,1,0:T(8,128)S(1)}, f32[16,40,128]{2,1,0:T(8,128)S(1)}, u32[]{:S(2)}, u32[]{:S(2)}) %collective-permute-start.1) | collective-permute-done | bytes 327712 | tf_op jit(solution)/shard_map/ppermute | solution.py:522
  71.2 0.9 shard_map.106
  72.2 10.8 %all_to_all.33.theta_ref = f32[16,8,128]{2,1,0:T(8,128)S(1)} all-to-all(f32[16,8,128]{2,1,0:T(8,128)S(1)} %get-tuple-element.39), channel_id=1, replica_groups=mesh['sky'=16,'band'=2] {'sky'}, dimensions={0} | all-to-all | bytes 131072 | tf_op jit(solution)/shard_map/all_to_all | solution.py:545
  83.0 4.9 %shard_map.107 = f32[16,40,128]{2,1,0:T(8,128)S(1)} custom-call(f32[16,8,128]{2,1,0:T(8,128)S(1)} %all_to_all.33.theta_ref, bf16[1024,256]{1,0:T(8,128)(2,1)S(1)} %get-tuple-element.25.hot_ref, bf16[1024,512]{1,0:T(8,128)(2,1)S(1)} %get-tuple-element.26.blend_ref, f32[8,256]{1,0:T(8,128)S(1)} %get-tuple-element.27.gain_ref, ...), custom_call_target="tpu_custom_call" | custom-call | tf_op jit(solution)/shard_map/pallas_call | solution.py:518
  87.9 13.2 %all_to_all.34.refs_0_ = f32[16,40,128]{2,1,0:T(8,128)S(1)} all-to-all(f32[16,40,128]{2,1,0:T(8,128)S(1)} %shard_map.107), channel_id=1, replica_groups=mesh['sky'=16,'band'=2] {'sky'}, dimensions={0} | all-to-all | bytes 655360 | tf_op jit(solution)/shard_map/all_to_all | solution.py:521
  101.0 0.0 collective-permute-start.2
  101.0 1.6 %collective-permute-done.2.refs_1_ = f32[16,40,128]{2,1,0:T(8,128)S(1)} collective-permute-done((f32[16,40,128]{2,1,0:T(8,128)S(1)}, f32[16,40,128]{2,1,0:T(8,128)S(1)}, u32[]{:S(2)}, u32[]{:S(2)}) %collective-permute-start.2) | collective-permute-done | bytes 327712 | tf_op jit(solution)/shard_map/ppermute | solution.py:522
  102.6 1.5 %shard_map.108 = f32[16,64]{1,0:T(8,128)} custom-call(f32[16,40,128]{2,1,0:T(8,128)S(1)} %all_to_all.34.refs_0_, f32[16,40,128]{2,1,0:T(8,128)S(1)} %collective-permute-done.2.refs_1_, bf16[64,512]{1,0:T(8,128)(2,1)S(1)} %get-tuple-element.37.refs_2_, bf16[272,256]{1,0:T(8,128)(2,1)S(1)} %get-tuple-element.35.refs_2_.refs_3_, ...), custom_call_target="tpu_custom_call" | custom-call | tf_op jit(solution)/shard_map/pallas_call | solution.py:540
Async XLA Ops:
  1.5 16.2 %all-to-all-start = ((f32[16,16,128]{2,1,0:T(8,128)}), f32[16,16,128]{2,1,0:T(8,128)S(1)}, u32[]{:S(2)}, u32[]{:S(2)}) async-start(f32[16,16,128]{2,1,0:T(8,128)} %shard_map.100), calls=%async_computation | async-start | bytes 262144 | tf_op jit(solution)/shard_map/all_to_all | solution.py:464
  19.6 19.9 %copy-start = (f32[16,64]{1,0:T(8,128)S(1)}, f32[16,64]{1,0:T(8,128)}, u32[]{:S(2)}) copy-start(f32[16,64]{1,0:T(8,128)} %refs_5_.3) | copy-start | bytes 12292
  37.9 1.6 %collective-permute-start = (f32[16,40,128]{2,1,0:T(8,128)S(1)}, f32[16,40,128]{2,1,0:T(8,128)S(1)}, u32[]{:S(2)}, u32[]{:S(2)}) collective-permute-start(f32[16,40,128]{2,1,0:T(8,128)S(1)} %all_to_all.30.refs_0_), channel_id=1, source_target_pairs={{0,1},{1,0},{2,3},{3,2},{4,5},{5,4},{6,7},{7,6},{8,9},{9,8},{10,11... | collective-permute-start | bytes 983048 | tf_op jit(solution)/shard_map/ppermute | solution.py:522
  69.6 1.6 %collective-permute-start.1 = (f32[16,40,128]{2,1,0:T(8,128)S(1)}, f32[16,40,128]{2,1,0:T(8,128)S(1)}, u32[]{:S(2)}, u32[]{:S(2)}) collective-permute-start(f32[16,40,128]{2,1,0:T(8,128)S(1)} %all_to_all.32.refs_0_), channel_id=1, source_target_pairs={{0,1},{1,0},{2,3},{3,2},{4,5},{5,4},{6,7},{7,6},{8,9},{9,8},{10,11... | collective-permute-start | bytes 983048 | tf_op jit(solution)/shard_map/ppermute | solution.py:522
  101.0 1.6 %collective-permute-start.2 = (f32[16,40,128]{2,1,0:T(8,128)S(1)}, f32[16,40,128]{2,1,0:T(8,128)S(1)}, u32[]{:S(2)}, u32[]{:S(2)}) collective-permute-start(f32[16,40,128]{2,1,0:T(8,128)S(1)} %all_to_all.34.refs_0_), channel_id=1, source_target_pairs={{0,1},{1,0},{2,3},{3,2},{4,5},{5,4},{6,7},{7,6},{8,9},{9,8},{10,11... | collective-permute-start | bytes 983048 | tf_op jit(solution)/shard_map/ppermute | solution.py:522

commit v4 on v3

--- a/solution.py
+++ b/solution.py
@@ -16,6 +16,7 @@
 
 LANES = 128
 GROUP = 32
+SUB = 4
 VMEM_LIMIT = 24 * 1024 * 1024
 
 f32 = jnp.float32
@@ -163,7 +164,10 @@
     before = iota((stamps, stamps), 0) < iota((stamps, stamps), 1)
     rank = jnp.sum(jnp.where(before & (along == along.T), 1.0, 0.0), axis=0, keepdims=True)
     owner_ref[...] = jnp.broadcast_to(dest * obj_dev + obj, owner_ref.shape)
-    place = dest * cap + rank.astype(jnp.int32)
+    half = cap // 2
+    rank = rank.astype(jnp.int32)
+    given = jnp.where(rank >= half, 1, 0) != lax.axis_index("band")
+    place = (dest + jnp.where(given, n_sky, 0)) * half + lax.rem(rank, half)
     sel_ref[...] = jnp.where(iota((total, stamps), 0) == place, 1.0, 0.0).astype(bf16)
     chunk = 256
 
@@ -249,13 +253,15 @@
     pair_ref,
     sel_ref,
     wide_ref,
-    out_ref,
+    keep_ref,
+    give_ref,
     amp_ref,
     acc_ref,
     proj_ref,
     lit_ref,
+    rows_ref,
 ):
-    n_sky, cap, fold, chunk, extra = sizes
+    n_sky, half, chunk, extra = sizes
     bands, stamps, pix = pix_ref.shape
     size_k = tpl_ref.shape[1] // 2
     steps = [
@@ -319,16 +325,17 @@
     )
     t1, t2, t3 = split3(terms)
     sel = sel_ref[...]
-    rows = dot(sel, t1) + (dot(sel, t2) + dot(sel, t3))
-    per = cap // fold
-    for d in range(n_sky):
-        base_row = d * cap
-        out_ref[d, 0:cap, :] = rows[base_row : base_row + cap, :LANES]
-        tail = rows[base_row : base_row + per, LANES:]
-        for g in range(1, fold):
-            at = base_row + g * per
-            tail = tail + pltpu.roll(rows[at : at + per, LANES:], g * GROUP, 1)
-        out_ref[d, cap : cap + per, :] = tail
+    rows_ref[...] = dot(sel, t1) + (dot(sel, t2) + dot(sel, t3))
+    groups = half // SUB
+    for part, out_ref in enumerate((keep_ref, give_ref)):
+        for d in range(n_sky):
+            at = (part * n_sky + d) * half
+            for g in range(groups):
+                line = rows_ref[at + g * SUB : at + (g + 1) * SUB, :]
+                out_ref[d, :, g * LANES : (g + 1) * LANES] = line[:, :LANES]
+                more = pltpu.roll(line[:, LANES:], g * GROUP, 1) if g else line[:, LANES:]
+                tail = tail + more if g else more
+            out_ref[d, :, groups * LANES :] = tail
 
 
 def solve_kernel(
@@ -344,18 +351,26 @@
     member_ref,
     rows_ref,
 ):
-    n_sky, cap, fold, n_band, tag, learn = sizes
-    per = cap // fold
+    n_sky, half, n_band, tag, learn = sizes
     size_k, obj_dev = theta_ref.shape
-    total = n_sky * cap
-    group = iota((per, LANES), 1) // GROUP
+    total = 2 * n_sky * half
+    groups = half // SUB
+    group = iota((SUB, LANES), 1) // GROUP
+    first = jnp.full((SUB, LANES), lax.axis_index("band")) == 0
     for d in range(n_sky):
-        both = recv_ref[d] + other_ref[d]
-        rows_ref[d * cap : d * cap + cap, 0:LANES] = both[0:cap]
-        tail = both[cap : cap + per]
-        for g in range(fold):
-            at = d * cap + g * per
-            rows_ref[at : at + per, LANES:] = jnp.where(group == g, tail, 0.0)
+        for g in range(groups + 1):
+            span = slice(g * LANES, (g + 1) * LANES)
+            mine, others = recv_ref[d, :, span], other_ref[d, :, span]
+            pair = (jnp.where(first, mine, others), jnp.where(first, others, mine))
+            for part, line in enumerate(pair):
+                at = (part * n_sky + d) * half
+                if g < groups:
+                    rows_ref[at + g * SUB : at + (g + 1) * SUB, 0:LANES] = line
+                else:
+                    for h in range(groups):
+                        rows_ref[at + h * SUB : at + (h + 1) * SUB, LANES:] = jnp.where(
+                            group == h, line, 0.0
+                        )
     p1, p2, p3 = split3(rows_ref[...])
     if learn:
         where_tag = jnp.where(column((8, 2 * LANES), LANES + tag), 1.0, 0.0).astype(bf16)
@@ -439,13 +454,13 @@
     size_k, obj_dev = theta_init.shape
     nei = nb_id.shape[1]
     cap = 2 * stamp_dev // n_sky
-    fold = max(1, min(LANES // GROUP, cap // 8))
+    half = cap // 2
     total = n_sky * cap
     n_all = n_sky * obj_dev
-    rows = cap + cap // fold
     extra = size_k * (size_k + 1) // 2 - LANES
     wide = LANES + -(-extra // 16) * 16
-    assert n_band == 2 and 2 * obj_dev == LANES and 0 <= extra and extra + size_k < GROUP
+    assert n_band == 2 and half % SUB == 0 and half // SUB <= LANES // GROUP
+    assert 2 * obj_dev == LANES and 0 <= extra and extra + size_k < GROUP
     shape = jax.ShapeDtypeStruct
     chunk = max(c for c in range(LANES, 1024, LANES) if pix % c == 0)
 
@@ -503,25 +518,28 @@
         "vvh",
     )(got, owner, hbm(pixels))
     terms = call(
-        functools.partial(terms_kernel, (n_sky, cap, fold, chunk, extra)),
-        shape((n_sky, rows, LANES), f32),
+        functools.partial(terms_kernel, (n_sky, half, chunk, extra)),
+        [shape((n_sky, SUB, (half // SUB + 1) * LANES), f32)] * 2,
         [
             pltpu.VMEM((size_k, n_all), f32),
             pltpu.VMEM((stamp_dev, 2 * LANES), f32),
             pltpu.VMEM((stamp_dev, LANES), f32),
             pltpu.VMEM((stamp_dev, 2 * size_k), bf16),
+            pltpu.VMEM((total, 2 * LANES), f32),
         ],
     )
+    swap = [(0, 1), (1, 0)]
     theta = theta_init
     member = None
     for sweep in range(ITERS):
-        sent = terms(
+        keep, give = terms(
             everyone, hot, blend, gain, base, tag, pixels, tpl, pair, sel, spread
         )
+        sent = keep + lax.ppermute(give, "band", swap)
         recv = lax.all_to_all(sent, "sky", 0, 0, tiled=True)
-        other = lax.ppermute(recv, "band", [(0, 1), (1, 0)])
+        other = lax.ppermute(recv, "band", swap)
         learn, last = sweep == 0, sweep + 1 == ITERS
-        sizes = (n_sky, cap, fold, n_band, extra + size_k, learn)
+        sizes = (n_sky, half, n_band, extra + size_k, learn)
 
         def solve(*refs, learn=learn, last=last, sizes=sizes):
             refs = list(refs)

time: 105 us -> 102 us (0.971)
  blocking collectives: 61.3 us -> 54.5 us
  waiting for transfers between devices: 9.03 us -> 12.5 us
    all_to_all x3, blocking collectives: 39.6 us -> 33 us  [local(): recv = lax.all_to_all(sent, 'sky', 0, 0, tiled=True)]
    ppermute x3 -> x6, waiting for transfers between devices: 4.88 us -> 8.32 us  [the longest x3 4.18 us: local(): other = lax.ppermute(recv, 'band', swap)]
  transfers between devices with their start and end apart: 4 -> 7, of which waited for: 4 -> 7; matrix products, arithmetic and copies ran while one was open for 0% -> 0% of each run, Pallas kernels for 3% -> 4%
where the time goes in v4:
time: 102 us
  blocking collectives  54.5 us (53%)
  Pallas kernels  25.9 us (25%)
  waiting for transfers between devices  12.5 us (12%)
  starting transfers between devices  8.57 us (8%)
    all_to_all x3, blocking collectives, local(): recv = lax.all_to_all(sent, 'sky', 0, 0, tiled=True)  33 us
    all_to_all x2, blocking collectives, local(): everyone = lax.all_to_all(outs[0], 'sky', 0, 0, tiled=True)  21.5 us
    pallas_call x3, Pallas kernels, local(): terms(everyone, hot, blend, gain, base, tag, pixels, tpl, pair, sel, spread)  14.8 us
    all_to_all x1, starting transfers between devices, local(): got = lax.all_to_all(payload, 'sky', 0, 0, tiled=True)  8.35 us
    ppermute x3, waiting for transfers between devices, local(): other = lax.ppermute(recv, 'band', swap)  4.18 us
    ppermute x3, waiting for transfers between devices, local(): sent = keep + lax.ppermute(give, 'band', swap)  4.14 us
    all_to_all x1, waiting for transfers between devices, local(): got = lax.all_to_all(payload, 'sky', 0, 0, tiled=True)  4.14 us
    pallas_call x3, Pallas kernels, local(): outs = call(solve, outs, [pltpu.VMEM((total, 2 * LANES), f32)])(*given)  4.02 us
  transfers between devices with their start and end apart: 7, of which 7 were waited for; matrix products, arithmetic and copies ran while one was open for 0% of the time, Pallas kernels for 4%

profile of v4, /device:TPU:0, one launch (start us, length us, event | category | flops | bytes accessed | tf_op | source)
XLA Modules:
  0.0 101.8 jit_solution(192159668981074434)
XLA Ops:
  0.0 1.5 %shard_map.100 = f32[16,16,128]{2,1,0:T(8,128)} custom-call(f32[16,64]{1,0:T(8,128)} %refs_5_.3, s32[4,64]{1,0:T(4,128)} %bitcast.6, f32[4,64]{1,0:T(4,128)} %bitcast.7), custom_call_target="tpu_custom_call" | custom-call | tf_op jit(solution)/shard_map/pallas_call | solution.py:468
  1.5 8.4 %all-to-all-start = ((f32[16,16,128]{2,1,0:T(8,128)}), f32[16,16,128]{2,1,0:T(8,128)S(1)}, u32[]{:S(2)}, u32[]{:S(2)}) async-start(f32[16,16,128]{2,1,0:T(8,128)} %shard_map.100), calls=%async_computation | async-start | bytes 262144 | tf_op jit(solution)/shard_map/all_to_all | solution.py:479
  9.8 3.6 %shard_map.101 = (bf16[3,32,2304]{2,1,0:T(8,128)(2,1)S(1)}, bf16[3,144,2304]{2,1,0:T(8,128)(2,1)S(1)}, bf16[512,256]{1,0:T(8,128)(2,1)S(1)}, bf16[48,512]{1,0:T(...) custom-call(s32[1,256]{1,0:T(1,128)} %bitcast.8, ...), custom_call_target="tpu_custom_call" | custom-call | tf_op jit(solution)/shard_map/pallas_call | solution.py:480
  13.5 4.1 %all-to-all-done.got_ref = f32[16,16,128]{2,1,0:T(8,128)S(1)} async-done(((f32[16,16,128]{2,1,0:T(8,128)}), f32[16,16,128]{2,1,0:T(8,128)S(1)}, u32[]{:S(2)}, u32[]{:S(2)}) %all-to-all-start) | async-done | bytes 131104 | tf_op jit(solution)/shard_map/all_to_all | solution.py:479
  17.6 2.0 %shard_map.102 = (f32[16,8,128]{2,1,0:T(8,128)S(1)}, bf16[1024,256]{1,0:T(8,128)(2,1)S(1)}, bf16[1024,512]{1,0:T(8,128)(2,1)S(1)}, bf16[3,256,2304]{2,1,0:T(8,128)(2,1)S(1)}) custom-call(f32[16,16,128]{2,1,0:T(8,128)S(1)} %all-to-all-done.got_ref, s32[8,256]{1,0:T(8,128)S(1)} %get-tuple-element.29.owner_ref, bf16[3,256,2304]{2,1,0:T(8,128)(2,1)} %bitcast.5), custom_call_target="tpu_custom_call" | custom-call | tf_op jit(solution)/shard_map/pallas_call | solution.py:509
  19.7 4.9 %shard_map.103 = (f32[16,4,640]{2,1,0:T(4,128)S(1)}, f32[16,4,640]{2,1,0:T(4,128)S(1)}) custom-call(f32[16,8,128]{2,1,0:T(8,128)S(1)} %get-tuple-element.30.theta_ref, bf16[1024,256]{1,0:T(8,128)(2,1)S(1)} %get-tuple-element.31.hot_ref, bf16[1024,512]{1,0:T(8,128)(2,1)S(1)} %get-tuple-element.32.blend_ref, f32[8,256]{1,0:T(8,128)S(1)} %get-tuple-element.33.gain_ref, ...), custom_call_target="tpu_custom_call" | custom-call | tf_op jit(solution)/shard_map/pallas_call | solution.py:535
  24.6 0.1 collective-permute-start
  24.7 1.4 %collective-permute-done = f32[16,4,640]{2,1,0:T(4,128)S(1)} collective-permute-done((f32[16,4,640]{2,1,0:T(4,128)S(1)}, f32[16,4,640]{2,1,0:T(4,128)S(1)}, u32[]{:S(2)}, u32[]{:S(2)}) %collective-permute-start) | collective-permute-done | bytes 163872 | tf_op jit(solution)/shard_map/ppermute | solution.py:538
  26.1 11.0 %all_to_all.30.refs_0_ = f32[16,4,640]{2,1,0:T(4,128)S(1)} all-to-all(f32[16,4,640]{2,1,0:T(4,128)S(1)} %add.9), channel_id=1, replica_groups=mesh['sky'=16,'band'=2] {'sky'}, dimensions={0} | all-to-all | bytes 327680 | tf_op jit(solution)/shard_map/all_to_all | solution.py:539
  37.1 1.4 %collective-permute-done.1.refs_1_ = f32[16,4,640]{2,1,0:T(4,128)S(1)} collective-permute-done((f32[16,4,640]{2,1,0:T(4,128)S(1)}, f32[16,4,640]{2,1,0:T(4,128)S(1)}, u32[]{:S(2)}, u32[]{:S(2)}) %collective-permute-start.1) | collective-permute-done | bytes 163872 | tf_op jit(solution)/shard_map/ppermute | solution.py:540
  38.5 1.3 %shard_map.104 = (f32[16,8,128]{2,1,0:T(8,128)S(1)}, f32[16,64]{1,0:T(8,128)S(1)}, bf16[64,512]{1,0:T(8,128)(2,1)S(1)}) custom-call(f32[16,4,640]{2,1,0:T(4,128)S(1)} %all_to_all.30.refs_0_, f32[16,4,640]{2,1,0:T(4,128)S(1)} %collective-permute-done.1.refs_1_, bf16[272,256]{1,0:T(8,128)(2,1)S(1)} %get-tuple-element.43.refs_2_.refs_3_, f32[16,64]{1,0:T(8,128)S(1)} %copy-done, ...), custom_call_target="tpu_custom_call" | custom-call | tf_op jit(solution)/shard_map/pallas_call | solution.py:558
  39.9 10.7 %all_to_all.31.theta_ref = f32[16,8,128]{2,1,0:T(8,128)S(1)} all-to-all(f32[16,8,128]{2,1,0:T(8,128)S(1)} %get-tuple-element.44), channel_id=1, replica_groups=mesh['sky'=16,'band'=2] {'sky'}, dimensions={0} | all-to-all | bytes 131072 | tf_op jit(solution)/shard_map/all_to_all | solution.py:563
  50.6 4.9 %shard_map.105 = (f32[16,4,640]{2,1,0:T(4,128)S(1)}, f32[16,4,640]{2,1,0:T(4,128)S(1)}) custom-call(f32[16,8,128]{2,1,0:T(8,128)S(1)} %all_to_all.31.theta_ref, bf16[1024,256]{1,0:T(8,128)(2,1)S(1)} %get-tuple-element.31.hot_ref, bf16[1024,512]{1,0:T(8,128)(2,1)S(1)} %get-tuple-element.32.blend_ref, f32[8,256]{1,0:T(8,128)S(1)} %get-tuple-element.33.gain_ref, ...), custom_call_target="tpu_custom_call" | custom-call | tf_op jit(solution)/shard_map/pallas_call | solution.py:535
  55.6 1.4 %collective-permute-done.2 = f32[16,4,640]{2,1,0:T(4,128)S(1)} collective-permute-done((f32[16,4,640]{2,1,0:T(4,128)S(1)}, f32[16,4,640]{2,1,0:T(4,128)S(1)}, u32[]{:S(2)}, u32[]{:S(2)}) %collective-permute-start.2) | collective-permute-done | bytes 163872 | tf_op jit(solution)/shard_map/ppermute | solution.py:538
  57.0 11.0 %all_to_all.32.refs_0_ = f32[16,4,640]{2,1,0:T(4,128)S(1)} all-to-all(f32[16,4,640]{2,1,0:T(4,128)S(1)} %add.10), channel_id=1, replica_groups=mesh['sky'=16,'band'=2] {'sky'}, dimensions={0} | all-to-all | bytes 327680 | tf_op jit(solution)/shard_map/all_to_all | solution.py:539
  68.1 1.4 %collective-permute-done.3.refs_1_ = f32[16,4,640]{2,1,0:T(4,128)S(1)} collective-permute-done((f32[16,4,640]{2,1,0:T(4,128)S(1)}, f32[16,4,640]{2,1,0:T(4,128)S(1)}, u32[]{:S(2)}, u32[]{:S(2)}) %collective-permute-start.3) | collective-permute-done | bytes 163872 | tf_op jit(solution)/shard_map/ppermute | solution.py:540
  69.5 1.1 %shard_map.106 = (f32[16,8,128]{2,1,0:T(8,128)S(1)}, f32[16,64]{1,0:T(8,128)S(1)}) custom-call(f32[16,4,640]{2,1,0:T(4,128)S(1)} %all_to_all.32.refs_0_, f32[16,4,640]{2,1,0:T(4,128)S(1)} %collective-permute-done.3.refs_1_, bf16[64,512]{1,0:T(8,128)(2,1)S(1)} %get-tuple-element.47.refs_2_, bf16[272,256]{1,0:T(8,128)(2,1)S(1)} %get-tuple-element.43.refs_2_.refs_3_, ...), custom_call_target="tpu_custom_call" | custom-call | tf_op jit(solution)/shard_map/pallas_call | solution.py:558
  70.5 10.8 %all_to_all.33.theta_ref = f32[16,8,128]{2,1,0:T(8,128)S(1)} all-to-all(f32[16,8,128]{2,1,0:T(8,128)S(1)} %get-tuple-element.49), channel_id=1, replica_groups=mesh['sky'=16,'band'=2] {'sky'}, dimensions={0} | all-to-all | bytes 131072 | tf_op jit(solution)/shard_map/all_to_all | solution.py:563
  81.3 4.9 %shard_map.107 = (f32[16,4,640]{2,1,0:T(4,128)S(1)}, f32[16,4,640]{2,1,0:T(4,128)S(1)}) custom-call(f32[16,8,128]{2,1,0:T(8,128)S(1)} %all_to_all.33.theta_ref, bf16[1024,256]{1,0:T(8,128)(2,1)S(1)} %get-tuple-element.31.hot_ref, bf16[1024,512]{1,0:T(8,128)(2,1)S(1)} %get-tuple-element.32.blend_ref, f32[8,256]{1,0:T(8,128)S(1)} %get-tuple-element.33.gain_ref, ...), custom_call_target="tpu_custom_call" | custom-call | tf_op jit(solution)/shard_map/pallas_call | solution.py:535
  86.2 0.1 collective-permute-start.4
  86.3 1.4 %collective-permute-done.4 = f32[16,4,640]{2,1,0:T(4,128)S(1)} collective-permute-done((f32[16,4,640]{2,1,0:T(4,128)S(1)}, f32[16,4,640]{2,1,0:T(4,128)S(1)}, u32[]{:S(2)}, u32[]{:S(2)}) %collective-permute-start.4) | collective-permute-done | bytes 163872 | tf_op jit(solution)/shard_map/ppermute | solution.py:538
  87.7 11.0 %all_to_all.34.refs_0_ = f32[16,4,640]{2,1,0:T(4,128)S(1)} all-to-all(f32[16,4,640]{2,1,0:T(4,128)S(1)} %add.11), channel_id=1, replica_groups=mesh['sky'=16,'band'=2] {'sky'}, dimensions={0} | all-to-all | bytes 327680 | tf_op jit(solution)/shard_map/all_to_all | solution.py:539
  98.7 1.4 %collective-permute-done.5.refs_1_ = f32[16,4,640]{2,1,0:T(4,128)S(1)} collective-permute-done((f32[16,4,640]{2,1,0:T(4,128)S(1)}, f32[16,4,640]{2,1,0:T(4,128)S(1)}, u32[]{:S(2)}, u32[]{:S(2)}) %collective-permute-start.5) | collective-permute-done | bytes 163872 | tf_op jit(solution)/shard_map/ppermute | solution.py:540
  100.1 1.6 %shard_map.108 = f32[16,64]{1,0:T(8,128)} custom-call(f32[16,4,640]{2,1,0:T(4,128)S(1)} %all_to_all.34.refs_0_, f32[16,4,640]{2,1,0:T(4,128)S(1)} %collective-permute-done.5.refs_1_, bf16[64,512]{1,0:T(8,128)(2,1)S(1)} %get-tuple-element.47.refs_2_, bf16[272,256]{1,0:T(8,128)(2,1)S(1)} %get-tuple-element.43.refs_2_.refs_3_, ...), custom_call_target="tpu_custom_call" | custom-call | tf_op jit(solution)/shard_map/pallas_call | solution.py:558
  (9 shorter events, 0.2 us)
Async XLA Ops:
  1.5 16.2 %all-to-all-start = ((f32[16,16,128]{2,1,0:T(8,128)}), f32[16,16,128]{2,1,0:T(8,128)S(1)}, u32[]{:S(2)}, u32[]{:S(2)}) async-start(f32[16,16,128]{2,1,0:T(8,128)} %shard_map.100), calls=%async_computation | async-start | bytes 262144 | tf_op jit(solution)/shard_map/all_to_all | solution.py:479
  19.7 18.9 %copy-start = (f32[16,64]{1,0:T(8,128)S(1)}, f32[16,64]{1,0:T(8,128)}, u32[]{:S(2)}) copy-start(f32[16,64]{1,0:T(8,128)} %refs_5_.3) | copy-start | bytes 12292
  24.6 1.5 %collective-permute-start = (f32[16,4,640]{2,1,0:T(4,128)S(1)}, f32[16,4,640]{2,1,0:T(4,128)S(1)}, u32[]{:S(2)}, u32[]{:S(2)}) collective-permute-start(f32[16,4,640]{2,1,0:T(4,128)S(1)} %get-tuple-element.42), channel_id=1, source_target_pairs={{0,1},{1,0},{2,3},{3,2},{4,5},{5,4},{6,7},{7,6},{8,9},{9,8},{10,11... | collective-permute-start | bytes 491528 | tf_op jit(solution)/shard_map/ppermute | solution.py:538
  37.1 1.4 %collective-permute-start.1 = (f32[16,4,640]{2,1,0:T(4,128)S(1)}, f32[16,4,640]{2,1,0:T(4,128)S(1)}, u32[]{:S(2)}, u32[]{:S(2)}) collective-permute-start(f32[16,4,640]{2,1,0:T(4,128)S(1)} %all_to_all.30.refs_0_), channel_id=1, source_target_pairs={{0,1},{1,0},{2,3},{3,2},{4,5},{5,4},{6,7},{7,6},{8,9},{9,8},{10,11... | collective-permute-start | bytes 491528 | tf_op jit(solution)/shard_map/ppermute | solution.py:540
  55.5 1.5 %collective-permute-start.2 = (f32[16,4,640]{2,1,0:T(4,128)S(1)}, f32[16,4,640]{2,1,0:T(4,128)S(1)}, u32[]{:S(2)}, u32[]{:S(2)}) collective-permute-start(f32[16,4,640]{2,1,0:T(4,128)S(1)} %get-tuple-element.46), channel_id=1, source_target_pairs={{0,1},{1,0},{2,3},{3,2},{4,5},{5,4},{6,7},{7,6},{8,9},{9,8},{10,11... | collective-permute-start | bytes 491528 | tf_op jit(solution)/shard_map/ppermute | solution.py:538
  68.1 1.4 %collective-permute-start.3 = (f32[16,4,640]{2,1,0:T(4,128)S(1)}, f32[16,4,640]{2,1,0:T(4,128)S(1)}, u32[]{:S(2)}, u32[]{:S(2)}) collective-permute-start(f32[16,4,640]{2,1,0:T(4,128)S(1)} %all_to_all.32.refs_0_), channel_id=1, source_target_pairs={{0,1},{1,0},{2,3},{3,2},{4,5},{5,4},{6,7},{7,6},{8,9},{9,8},{10,11... | collective-permute-start | bytes 491528 | tf_op jit(solution)/shard_map/ppermute | solution.py:540
  86.2 1.5 %collective-permute-start.4 = (f32[16,4,640]{2,1,0:T(4,128)S(1)}, f32[16,4,640]{2,1,0:T(4,128)S(1)}, u32[]{:S(2)}, u32[]{:S(2)}) collective-permute-start(f32[16,4,640]{2,1,0:T(4,128)S(1)} %get-tuple-element.51), channel_id=1, source_target_pairs={{0,1},{1,0},{2,3},{3,2},{4,5},{5,4},{6,7},{7,6},{8,9},{9,8},{10,11... | collective-permute-start | bytes 491528 | tf_op jit(solution)/shard_map/ppermute | solution.py:538
  98.7 1.4 %collective-permute-start.5 = (f32[16,4,640]{2,1,0:T(4,128)S(1)}, f32[16,4,640]{2,1,0:T(4,128)S(1)}, u32[]{:S(2)}, u32[]{:S(2)}) collective-permute-start(f32[16,4,640]{2,1,0:T(4,128)S(1)} %all_to_all.34.refs_0_), channel_id=1, source_target_pairs={{0,1},{1,0},{2,3},{3,2},{4,5},{5,4},{6,7},{7,6},{8,9},{9,8},{10,11... | collective-permute-start | bytes 491528 | tf_op jit(solution)/shard_map/ppermute | solution.py:540

commit v5 on v4

--- a/solution.py
+++ b/solution.py
@@ -61,27 +61,6 @@
     lane = iota(shape, 1)
     folded = jnp.where(lane < LANES, lane, LANES + lax.rem(lane, GROUP))
     return folded == m
-
-
-def pack_kernel(theta_hbm, nbi_hbm, nbw_hbm, pay_ref, theta_ref, nbi_ref, nbw_ref, sem):
-    n_sky = pay_ref.shape[0]
-    wait(
-        dma(
-            [
-                pltpu.make_async_copy(theta_hbm, theta_ref, sem.at[0]),
-                pltpu.make_async_copy(nbi_hbm, nbi_ref, sem.at[1]),
-                pltpu.make_async_copy(nbw_hbm, nbw_ref, sem.at[2]),
-            ]
-        )
-    )
-    half = theta_ref.shape[0] // 2
-    theta = theta_ref[...]
-    folded = jnp.concatenate([theta[:half], theta[half:]], axis=1)
-    side = jnp.concatenate([nbi_ref[...].astype(f32), nbw_ref[...]], axis=1)
-    side = jnp.concatenate([side, jnp.zeros((8 - side.shape[0], LANES), f32)], axis=0)
-    for d in range(n_sky):
-        pay_ref[d, 0:8, :] = folded
-        pay_ref[d, 8:16, :] = side
 
 
 def ready_kernel(
@@ -92,6 +71,12 @@
     invvar_hbm,
     phi_hbm,
     psi_hbm,
+    theta_hbm,
+    nbi_hbm,
+    nbw_hbm,
+    pix_hbm,
+    pay_ref,
+    pix_ref,
     tpl_ref,
     pair_ref,
     sel_ref,
@@ -105,9 +90,12 @@
     obj_ref,
     gain_low_ref,
     invvar_ref,
+    theta_ref,
+    nbi_ref,
+    nbw_ref,
     sem,
 ):
-    n_sky, cap, obj_dev, extra = sizes
+    n_sky, cap, obj_dev, extra, chunk = sizes
     bands, size_k, pix = phi_hbm.shape
     stamps = dest_ref.shape[1]
     total = n_sky * cap
@@ -118,8 +106,13 @@
         pltpu.make_async_copy(obj_hbm, obj_ref, sem.at[3]),
         pltpu.make_async_copy(gain_hbm, gain_low_ref, sem.at[4]),
         pltpu.make_async_copy(invvar_hbm, invvar_ref, sem.at[5]),
+        pltpu.make_async_copy(theta_hbm, theta_ref, sem.at[6]),
+        pltpu.make_async_copy(nbi_hbm, nbi_ref, sem.at[7]),
+        pltpu.make_async_copy(nbw_hbm, nbw_ref, sem.at[8]),
     ]
+    last = [pltpu.make_async_copy(pix_hbm, pix_ref, sem.at[9])]
     dma(first)
+    dma(last)
 
     pairs = LANES + extra
     shape = (pair_ref.shape[1], size_k)
@@ -150,6 +143,13 @@
     full_ref[...] = jnp.where(column(shape, m), 1.0, 0.0).astype(bf16)
 
     wait(first)
+    theta = theta_ref[...]
+    folded = jnp.concatenate([theta[: size_k // 2], theta[size_k // 2 :]], axis=1)
+    side = jnp.concatenate([nbi_ref[...].astype(f32), nbw_ref[...]], axis=1)
+    side = jnp.concatenate([side, jnp.zeros((8 - side.shape[0], LANES), f32)], axis=0)
+    for d in range(n_sky):
+        pay_ref[d, 0:8, :] = folded
+        pay_ref[d, 8:16, :] = side
     dest = dest_ref[...]
     obj = obj_ref[...]
     gain = gain_low_ref[...].astype(f32).reshape(1, stamps)
@@ -169,16 +169,12 @@
     given = jnp.where(rank >= half, 1, 0) != lax.axis_index("band")
     place = (dest + jnp.where(given, n_sky, 0)) * half + lax.rem(rank, half)
     sel_ref[...] = jnp.where(iota((total, stamps), 0) == place, 1.0, 0.0).astype(bf16)
-    chunk = 256
-
-    def step(c, carry):
-        px = pl.ds(pl.multiple_of(c * chunk, chunk), chunk)
-        for b in range(bands):
+    for b in range(bands):
+        for c in range(pix // chunk):
+            px = slice(c * chunk, (c + 1) * chunk)
             phi = tpl_ref[b, 0:size_k, px]
             pair_ref[b, :, px] = (dot(lows, phi) * dot(highs, phi)).astype(bf16)
-        return carry
-
-    lax.fori_loop(0, pix // chunk, step, 0)
+    wait(last)
 
 
 def unfold(ref, rows, lane, i, left):
@@ -188,20 +184,9 @@
     return jnp.where(lane < LANES // 2, pltpu.roll(x, LANES // 2, 1), y)
 
 
-def index_kernel(
-    nei, got_ref, owner_ref, pix_hbm, theta_ref, hot_ref, blend_ref, pix_ref, table_ref, sem
-):
-    bands, stamps = pix_ref.shape[:2]
-    half = stamps // 2
-    parts = [(b, slice(h * half, (h + 1) * half)) for b in range(bands) for h in range(2)]
-    load = dma(
-        [
-            pltpu.make_async_copy(pix_hbm.at[b, rows], pix_ref.at[b, rows], sem.at[i])
-            for i, (b, rows) in enumerate(parts)
-        ]
-    )
+def index_kernel(nei, got_ref, owner_ref, theta_ref, hot_ref, blend_ref, table_ref):
     n_sky = got_ref.shape[0]
-    n_all = hot_ref.shape[0]
+    n_all, stamps = hot_ref.shape
     block = LANES
     owner = owner_ref[0:1, :]
 
@@ -237,7 +222,6 @@
         return carry
 
     lax.fori_loop(0, n_all // block, blend, 0)
-    wait(load)
 
 
 def terms_kernel(
@@ -465,21 +449,11 @@
     chunk = max(c for c in range(LANES, 1024, LANES) if pix % c == 0)
 
     pixels = jnp.transpose(stamps, (1, 0, 2))
-    payload = call(
-        pack_kernel,
-        shape((n_sky, 16, LANES), f32),
-        [
-            pltpu.VMEM((size_k, obj_dev), f32),
-            pltpu.VMEM((nei, obj_dev), jnp.int32),
-            pltpu.VMEM((nei, obj_dev), f32),
-            pltpu.SemaphoreType.DMA((3,)),
-        ],
-        "hhh",
-    )(hbm(theta_init), hbm(nb_id.T), hbm(nb_weight.T))
-    got = lax.all_to_all(payload, "sky", 0, 0, tiled=True)
-    tpl, pair, sel, spread, full, base, tag, gain, owner = call(
-        functools.partial(ready_kernel, (n_sky, cap, obj_dev, extra)),
+    payload, pixels, tpl, pair, sel, spread, full, base, tag, gain, owner = call(
+        functools.partial(ready_kernel, (n_sky, cap, obj_dev, extra, chunk)),
         (
+            shape((n_sky, 16, LANES), f32),
+            shape((bands, stamp_dev, pix), bf16),
             shape((bands, 2 * size_k, pix), bf16),
             shape((bands, wide, pix), bf16),
             shape((total, stamp_dev), bf16),
@@ -495,9 +469,12 @@
             pltpu.VMEM((1, stamp_dev), jnp.int32),
             pltpu.VMEM((stamp_dev,), bf16),
             pltpu.VMEM((stamp_dev,), bf16),
-            pltpu.SemaphoreType.DMA((6,)),
+            pltpu.VMEM((size_k, obj_dev), f32),
+            pltpu.VMEM((nei, obj_dev), jnp.int32),
+            pltpu.VMEM((nei, obj_dev), f32),
+            pltpu.SemaphoreType.DMA((10,)),
         ],
-        "hhhhhh",
+        "h" * 10,
     )(
         hbm(stamp_dest.T),
         hbm(stamp_obj[None, :]),
@@ -505,18 +482,21 @@
         hbm(stamp_invvar),
         hbm(phi_tpl),
         hbm(psi_tpl),
+        hbm(theta_init),
+        hbm(nb_id.T),
+        hbm(nb_weight.T),
+        hbm(pixels),
     )
-    everyone, hot, blend, pixels = call(
+    got = lax.all_to_all(payload, "sky", 0, 0, tiled=True)
+    everyone, hot, blend = call(
         functools.partial(index_kernel, nei),
         (
             shape((n_sky, 8, LANES), f32),
             shape((n_all, stamp_dev), bf16),
             shape((n_all, 2 * stamp_dev), bf16),
-            shape((bands, stamp_dev, pix), bf16),
         ),
-        [pltpu.VMEM((16, n_all), f32), pltpu.SemaphoreType.DMA((2 * bands,))],
-        "vvh",
-    )(got, owner, hbm(pixels))
+        [pltpu.VMEM((16, n_all), f32)],
+    )(got, owner)
     terms = call(
         functools.partial(terms_kernel, (n_sky, half, chunk, extra)),
         [shape((n_sky, SUB, (half // SUB + 1) * LANES), f32)] * 2,

time: 102 us -> 102 us (level)
  blocking collectives: 54.5 us -> 70.5 us
  starting transfers between devices: 8.57 us -> 0.22 us
  waiting for transfers between devices: 12.5 us -> 8.32 us
  Pallas kernels: 25.9 us -> 22.6 us
    all_to_all x0 -> x1, blocking collectives: none -> 15.9 us  [local(): got = lax.all_to_all(payload, 'sky', 0, 0, tiled=True)]
    all_to_all x1 -> x0, starting transfers between devices: 8.35 us -> none  [local(): got = lax.all_to_all(payload, 'sky', 0, 0, tiled=True)]
    all_to_all x1 -> x0, waiting for transfers between devices: 4.14 us -> none  [local(): got = lax.all_to_all(payload, 'sky', 0, 0, tiled=True)]
    pallas_call x2 -> x1, Pallas kernels: 5.12 us -> 2.43 us  [local(): call(functools.partial(ready_kernel, (n_sky, cap, obj_dev, extra, chunk))...]
    pallas_call x1, Pallas kernels: 2 us -> 0.96 us  [local(): call(functools.partial(index_kernel, nei), (shape((n_sky, 8, LANES), f32)...]
  transfers between devices with their start and end apart: 7 -> 6, of which waited for: 7 -> 6; matrix products, arithmetic and copies ran while one was open for 0% -> 0% of each run, Pallas kernels for 4% -> 0%
where the time goes in v5:
time: 102 us
  blocking collectives  70.5 us (69%)
  Pallas kernels  22.6 us (22%)
  waiting for transfers between devices  8.32 us (8%)
    all_to_all x3, blocking collectives, local(): recv = lax.all_to_all(sent, 'sky', 0, 0, tiled=True)  33 us
    all_to_all x2, blocking collectives, local(): everyone = lax.all_to_all(outs[0], 'sky', 0, 0, tiled=True)  21.5 us
    all_to_all x1, blocking collectives, local(): got = lax.all_to_all(payload, 'sky', 0, 0, tiled=True)  15.9 us
    pallas_call x3, Pallas kernels, local(): terms(everyone, hot, blend, gain, base, tag, pixels, tpl, pair, sel, spread)  15.2 us
    ppermute x3, waiting for transfers between devices, local(): other = lax.ppermute(recv, 'band', swap)  4.18 us
    ppermute x3, waiting for transfers between devices, local(): sent = keep + lax.ppermute(give, 'band', swap)  4.14 us
    pallas_call x3, Pallas kernels, local(): outs = call(solve, outs, [pltpu.VMEM((total, 2 * LANES), f32)])(*given)  4.03 us
    pallas_call x1, Pallas kernels, local(): call(functools.partial(ready_kernel, (n_sky, cap, obj_dev, extra, chunk))...  2.43 us
  transfers between devices with their start and end apart: 6, of which 6 were waited for; matrix products, arithmetic and copies ran while one was open for 0% of the time, Pallas kernels for 0%

profile of v5, /device:TPU:0, one launch (start us, length us, event | category | flops | bytes accessed | tf_op | source)
XLA Modules:
  0.0 101.9 jit_solution(7581013496885565331)
XLA Ops:
  0.0 2.4 %shard_map.100 = (f32[16,16,128]{2,1,0:T(8,128)S(1)}, bf16[3,256,2304]{2,1,0:T(8,128)(2,1)S(1)}, bf16[3,32,2304]{2,1,0:T(8,128)(2,1)S(1)}, bf16[3,144,2304]{2,1,...) custom-call(s32[1,256]{1,0:T(1,128)} %bitcast.8, ...), custom_call_target="tpu_custom_call" | custom-call | tf_op jit(solution)/shard_map/pallas_call | solution.py:452
  2.4 15.9 %all_to_all.30.got_ref = f32[16,16,128]{2,1,0:T(8,128)S(1)} all-to-all(f32[16,16,128]{2,1,0:T(8,128)S(1)} %get-tuple-element.30), channel_id=1, replica_groups=mesh['sky'=16,'band'=2] {'sky'}, dimensions={0} | all-to-all | bytes 262144 | tf_op jit(solution)/shard_map/all_to_all | solution.py:490
  18.4 1.0 shard_map.101
  19.3 0.0 copy-start
  19.4 5.1 %shard_map.102 = (f32[16,4,640]{2,1,0:T(4,128)S(1)}, f32[16,4,640]{2,1,0:T(4,128)S(1)}) custom-call(f32[16,8,128]{2,1,0:T(8,128)S(1)} %get-tuple-element.32.theta_ref, bf16[1024,256]{1,0:T(8,128)(2,1)S(1)} %get-tuple-element.33.hot_ref, bf16[1024,512]{1,0:T(8,128)(2,1)S(1)} %get-tuple-element.34.blend_ref, f32[8,256]{1,0:T(8,128)S(1)} %get-tuple-element.35.gain_ref, ...), custom_call_target="tpu_custom_call" | custom-call | tf_op jit(solution)/shard_map/pallas_call | solution.py:515
  24.4 0.1 collective-permute-start
  24.5 1.4 %collective-permute-done = f32[16,4,640]{2,1,0:T(4,128)S(1)} collective-permute-done((f32[16,4,640]{2,1,0:T(4,128)S(1)}, f32[16,4,640]{2,1,0:T(4,128)S(1)}, u32[]{:S(2)}, u32[]{:S(2)}) %collective-permute-start) | collective-permute-done | bytes 163872 | tf_op jit(solution)/shard_map/ppermute | solution.py:518
  25.9 11.0 %all_to_all.31.refs_0_ = f32[16,4,640]{2,1,0:T(4,128)S(1)} all-to-all(f32[16,4,640]{2,1,0:T(4,128)S(1)} %add.9), channel_id=1, replica_groups=mesh['sky'=16,'band'=2] {'sky'}, dimensions={0} | all-to-all | bytes 327680 | tf_op jit(solution)/shard_map/all_to_all | solution.py:519
  37.0 1.4 %collective-permute-done.1.refs_1_ = f32[16,4,640]{2,1,0:T(4,128)S(1)} collective-permute-done((f32[16,4,640]{2,1,0:T(4,128)S(1)}, f32[16,4,640]{2,1,0:T(4,128)S(1)}, u32[]{:S(2)}, u32[]{:S(2)}) %collective-permute-start.1) | collective-permute-done | bytes 163872 | tf_op jit(solution)/shard_map/ppermute | solution.py:520
  38.4 1.3 %shard_map.103 = (f32[16,8,128]{2,1,0:T(8,128)S(1)}, f32[16,64]{1,0:T(8,128)S(1)}, bf16[64,512]{1,0:T(8,128)(2,1)S(1)}) custom-call(f32[16,4,640]{2,1,0:T(4,128)S(1)} %all_to_all.31.refs_0_, f32[16,4,640]{2,1,0:T(4,128)S(1)} %collective-permute-done.1.refs_1_, bf16[272,256]{1,0:T(8,128)(2,1)S(1)} %get-tuple-element.45.refs_2_.refs_3_, f32[16,64]{1,0:T(8,128)S(1)} %copy-done, ...), custom_call_target="tpu_custom_call" | custom-call | tf_op jit(solution)/shard_map/pallas_call | solution.py:538
  39.7 10.7 %all_to_all.32.theta_ref = f32[16,8,128]{2,1,0:T(8,128)S(1)} all-to-all(f32[16,8,128]{2,1,0:T(8,128)S(1)} %get-tuple-element.46), channel_id=1, replica_groups=mesh['sky'=16,'band'=2] {'sky'}, dimensions={0} | all-to-all | bytes 131072 | tf_op jit(solution)/shard_map/all_to_all | solution.py:543
  50.4 5.1 %shard_map.104 = (f32[16,4,640]{2,1,0:T(4,128)S(1)}, f32[16,4,640]{2,1,0:T(4,128)S(1)}) custom-call(f32[16,8,128]{2,1,0:T(8,128)S(1)} %all_to_all.32.theta_ref, bf16[1024,256]{1,0:T(8,128)(2,1)S(1)} %get-tuple-element.33.hot_ref, bf16[1024,512]{1,0:T(8,128)(2,1)S(1)} %get-tuple-element.34.blend_ref, f32[8,256]{1,0:T(8,128)S(1)} %get-tuple-element.35.gain_ref, ...), custom_call_target="tpu_custom_call" | custom-call | tf_op jit(solution)/shard_map/pallas_call | solution.py:515
  55.5 0.1 collective-permute-start.2
  55.6 1.4 %collective-permute-done.2 = f32[16,4,640]{2,1,0:T(4,128)S(1)} collective-permute-done((f32[16,4,640]{2,1,0:T(4,128)S(1)}, f32[16,4,640]{2,1,0:T(4,128)S(1)}, u32[]{:S(2)}, u32[]{:S(2)}) %collective-permute-start.2) | collective-permute-done | bytes 163872 | tf_op jit(solution)/shard_map/ppermute | solution.py:518
  57.0 11.0 %all_to_all.33.refs_0_ = f32[16,4,640]{2,1,0:T(4,128)S(1)} all-to-all(f32[16,4,640]{2,1,0:T(4,128)S(1)} %add.10), channel_id=1, replica_groups=mesh['sky'=16,'band'=2] {'sky'}, dimensions={0} | all-to-all | bytes 327680 | tf_op jit(solution)/shard_map/all_to_all | solution.py:519
  68.0 1.4 %collective-permute-done.3.refs_1_ = f32[16,4,640]{2,1,0:T(4,128)S(1)} collective-permute-done((f32[16,4,640]{2,1,0:T(4,128)S(1)}, f32[16,4,640]{2,1,0:T(4,128)S(1)}, u32[]{:S(2)}, u32[]{:S(2)}) %collective-permute-start.3) | collective-permute-done | bytes 163872 | tf_op jit(solution)/shard_map/ppermute | solution.py:520
  69.4 1.1 %shard_map.105 = (f32[16,8,128]{2,1,0:T(8,128)S(1)}, f32[16,64]{1,0:T(8,128)S(1)}) custom-call(f32[16,4,640]{2,1,0:T(4,128)S(1)} %all_to_all.33.refs_0_, f32[16,4,640]{2,1,0:T(4,128)S(1)} %collective-permute-done.3.refs_1_, bf16[64,512]{1,0:T(8,128)(2,1)S(1)} %get-tuple-element.49.refs_2_, bf16[272,256]{1,0:T(8,128)(2,1)S(1)} %get-tuple-element.45.refs_2_.refs_3_, ...), custom_call_target="tpu_custom_call" | custom-call | tf_op jit(solution)/shard_map/pallas_call | solution.py:538
  70.5 10.7 %all_to_all.34.theta_ref = f32[16,8,128]{2,1,0:T(8,128)S(1)} all-to-all(f32[16,8,128]{2,1,0:T(8,128)S(1)} %get-tuple-element.51), channel_id=1, replica_groups=mesh['sky'=16,'band'=2] {'sky'}, dimensions={0} | all-to-all | bytes 131072 | tf_op jit(solution)/shard_map/all_to_all | solution.py:543
  81.2 5.1 %shard_map.106 = (f32[16,4,640]{2,1,0:T(4,128)S(1)}, f32[16,4,640]{2,1,0:T(4,128)S(1)}) custom-call(f32[16,8,128]{2,1,0:T(8,128)S(1)} %all_to_all.34.theta_ref, bf16[1024,256]{1,0:T(8,128)(2,1)S(1)} %get-tuple-element.33.hot_ref, bf16[1024,512]{1,0:T(8,128)(2,1)S(1)} %get-tuple-element.34.blend_ref, f32[8,256]{1,0:T(8,128)S(1)} %get-tuple-element.35.gain_ref, ...), custom_call_target="tpu_custom_call" | custom-call | tf_op jit(solution)/shard_map/pallas_call | solution.py:515
  86.3 0.1 collective-permute-start.4
  86.4 1.4 %collective-permute-done.4 = f32[16,4,640]{2,1,0:T(4,128)S(1)} collective-permute-done((f32[16,4,640]{2,1,0:T(4,128)S(1)}, f32[16,4,640]{2,1,0:T(4,128)S(1)}, u32[]{:S(2)}, u32[]{:S(2)}) %collective-permute-start.4) | collective-permute-done | bytes 163872 | tf_op jit(solution)/shard_map/ppermute | solution.py:518
  87.8 11.0 %all_to_all.35.refs_0_ = f32[16,4,640]{2,1,0:T(4,128)S(1)} all-to-all(f32[16,4,640]{2,1,0:T(4,128)S(1)} %add.11), channel_id=1, replica_groups=mesh['sky'=16,'band'=2] {'sky'}, dimensions={0} | all-to-all | bytes 327680 | tf_op jit(solution)/shard_map/all_to_all | solution.py:519
  98.8 1.4 %collective-permute-done.5.refs_1_ = f32[16,4,640]{2,1,0:T(4,128)S(1)} collective-permute-done((f32[16,4,640]{2,1,0:T(4,128)S(1)}, f32[16,4,640]{2,1,0:T(4,128)S(1)}, u32[]{:S(2)}, u32[]{:S(2)}) %collective-permute-start.5) | collective-permute-done | bytes 163872 | tf_op jit(solution)/shard_map/ppermute | solution.py:520
  100.2 1.6 %shard_map.107 = f32[16,64]{1,0:T(8,128)} custom-call(f32[16,4,640]{2,1,0:T(4,128)S(1)} %all_to_all.35.refs_0_, f32[16,4,640]{2,1,0:T(4,128)S(1)} %collective-permute-done.5.refs_1_, bf16[64,512]{1,0:T(8,128)(2,1)S(1)} %get-tuple-element.49.refs_2_, bf16[272,256]{1,0:T(8,128)(2,1)S(1)} %get-tuple-element.45.refs_2_.refs_3_, ...), custom_call_target="tpu_custom_call" | custom-call | tf_op jit(solution)/shard_map/pallas_call | solution.py:538
  (7 shorter events, 0.1 us)
Async XLA Ops:
  19.3 19.0 %copy-start = (f32[16,64]{1,0:T(8,128)S(1)}, f32[16,64]{1,0:T(8,128)}, u32[]{:S(2)}) copy-start(f32[16,64]{1,0:T(8,128)} %refs_5_.3) | copy-start | bytes 12292
  24.4 1.5 %collective-permute-start = (f32[16,4,640]{2,1,0:T(4,128)S(1)}, f32[16,4,640]{2,1,0:T(4,128)S(1)}, u32[]{:S(2)}, u32[]{:S(2)}) collective-permute-start(f32[16,4,640]{2,1,0:T(4,128)S(1)} %get-tuple-element.44), channel_id=1, source_target_pairs={{0,1},{1,0},{2,3},{3,2},{4,5},{5,4},{6,7},{7,6},{8,9},{9,8},{10,11... | collective-permute-start | bytes 491528 | tf_op jit(solution)/shard_map/ppermute | solution.py:518
  37.0 1.4 %collective-permute-start.1 = (f32[16,4,640]{2,1,0:T(4,128)S(1)}, f32[16,4,640]{2,1,0:T(4,128)S(1)}, u32[]{:S(2)}, u32[]{:S(2)}) collective-permute-start(f32[16,4,640]{2,1,0:T(4,128)S(1)} %all_to_all.31.refs_0_), channel_id=1, source_target_pairs={{0,1},{1,0},{2,3},{3,2},{4,5},{5,4},{6,7},{7,6},{8,9},{9,8},{10,11... | collective-permute-start | bytes 491528 | tf_op jit(solution)/shard_map/ppermute | solution.py:520
  55.5 1.5 %collective-permute-start.2 = (f32[16,4,640]{2,1,0:T(4,128)S(1)}, f32[16,4,640]{2,1,0:T(4,128)S(1)}, u32[]{:S(2)}, u32[]{:S(2)}) collective-permute-start(f32[16,4,640]{2,1,0:T(4,128)S(1)} %get-tuple-element.48), channel_id=1, source_target_pairs={{0,1},{1,0},{2,3},{3,2},{4,5},{5,4},{6,7},{7,6},{8,9},{9,8},{10,11... | collective-permute-start | bytes 491528 | tf_op jit(solution)/shard_map/ppermute | solution.py:518
  68.0 1.4 %collective-permute-start.3 = (f32[16,4,640]{2,1,0:T(4,128)S(1)}, f32[16,4,640]{2,1,0:T(4,128)S(1)}, u32[]{:S(2)}, u32[]{:S(2)}) collective-permute-start(f32[16,4,640]{2,1,0:T(4,128)S(1)} %all_to_all.33.refs_0_), channel_id=1, source_target_pairs={{0,1},{1,0},{2,3},{3,2},{4,5},{5,4},{6,7},{7,6},{8,9},{9,8},{10,11... | collective-permute-start | bytes 491528 | tf_op jit(solution)/shard_map/ppermute | solution.py:520
  86.3 1.5 %collective-permute-start.4 = (f32[16,4,640]{2,1,0:T(4,128)S(1)}, f32[16,4,640]{2,1,0:T(4,128)S(1)}, u32[]{:S(2)}, u32[]{:S(2)}) collective-permute-start(f32[16,4,640]{2,1,0:T(4,128)S(1)} %get-tuple-element.53), channel_id=1, source_target_pairs={{0,1},{1,0},{2,3},{3,2},{4,5},{5,4},{6,7},{7,6},{8,9},{9,8},{10,11... | collective-permute-start | bytes 491528 | tf_op jit(solution)/shard_map/ppermute | solution.py:518
  98.8 1.4 %collective-permute-start.5 = (f32[16,4,640]{2,1,0:T(4,128)S(1)}, f32[16,4,640]{2,1,0:T(4,128)S(1)}, u32[]{:S(2)}, u32[]{:S(2)}) collective-permute-start(f32[16,4,640]{2,1,0:T(4,128)S(1)} %all_to_all.35.refs_0_), channel_id=1, source_target_pairs={{0,1},{1,0},{2,3},{3,2},{4,5},{5,4},{6,7},{7,6},{8,9},{9,8},{10,11... | collective-permute-start | bytes 491528 | tf_op jit(solution)/shard_map/ppermute | solution.py:520
